TPU v7x, 32 devices: a whole 2x2x4 slice. The times are simulated.
32 devices in a mesh: groups: 2 (over x), tm: 16 (over z, y, core).
Axes of the slice: x: 2, y: 2, z: 4, core: 2. Of those that a mesh axis runs over, the one named last changes fastest.
Arguments:
- states: bfloat16 [4096, 2, 1024], P('tm', 'groups'), parts along dimension 1, may hold values from -6 to 6
- goals: bfloat16 [4096, 2, 1024], P('tm', 'groups'), parts along dimension 1, may hold values from -6 to 6
- pos_offset: int32 [16, 2, 8], P('tm', 'groups'), parts along dimension 1, may hold values from 0 to 15
- neg_blocks: int32 [16, 2, 16], P('tm', 'groups'), parts along dimension 1, may hold values from 0 to 15
Outputs:
- loss_mean: float32 [2], P('groups'), parts along dimension 0
- grad_states: float32 [4096, 2, 1024], P('tm', 'groups'), parts along dimension 1
- grad_goals: float32 [4096, 2, 1024], P('tm', 'groups'), parts along dimension 1
There are 2 independent parts, one for each index of `groups`. A program takes and returns all parts, laid end to end along the dimension named above; each array names one. Nothing has to cross between parts.
All inputs are finite; a program needn't handle non-finite values.
Results may differ from a plain program's by a relative error of at most 0.012.
Values may be sent and summed in bfloat16 or wider, within the bound.
No kernel may reach another device: no remote copies, remote signals or barrier semaphores. Data moves between devices by JAX's collectives and lax.ppermute only.
A program may use at most 128 MiB of HBM per device.

v0:
```python
import math

import jax
import jax.numpy as jnp
from jax import lax
from jax.sharding import PartitionSpec as P

E = 1024
L = 256


def pair_weights(pos_offset, neg_blocks, row_first, row_count, col_count):
    block_count = row_count // L
    row_blocks = row_first // L + jnp.arange(block_count, dtype=jnp.int32)
    col_times = jnp.arange(col_count, dtype=jnp.int32)
    col_blocks = col_times // L
    targets = row_blocks[:, None, None] + pos_offset
    pos_count = jnp.sum((targets[..., None] == col_blocks).astype(jnp.float32), axis=2)
    neg_count = jnp.sum((neg_blocks[..., None] == col_blocks).astype(jnp.float32), axis=2)
    pos_count = jnp.repeat(jnp.swapaxes(pos_count, 0, 1), L, axis=1)
    neg_count = jnp.repeat(jnp.swapaxes(neg_count, 0, 1), L, axis=1)
    row_times = row_first + jnp.arange(row_count, dtype=jnp.int32)
    later_mask = (col_times[None, :] > row_times[:, None]).astype(jnp.float32)
    return (pos_count * later_mask, neg_count)


def score_terms(anchor_rows, goal_rows, pos_weight, neg_weight):
    inv_root = 1.0 / math.sqrt(E)
    scores = (
        jnp.einsum("qte,kte->tqk", anchor_rows, goal_rows, preferred_element_type=jnp.float32)
        * inv_root
    )
    loss_sum = jnp.sum(pos_weight * jax.nn.softplus(-scores) + neg_weight * jax.nn.softplus(scores))
    slopes = neg_weight * jax.nn.sigmoid(scores) - pos_weight * jax.nn.sigmoid(-scores)
    return (loss_sum, (slopes * inv_root).astype(jnp.bfloat16))


def per_device(states, goals, pos_offset, neg_blocks):
    row_count = states.shape[0]
    traj_count = states.shape[1]
    steps_all = row_count * lax.axis_size("tm")
    row_first = lax.axis_index("tm") * row_count
    goal_piece = lax.all_gather(goals, "tm", axis=0, tiled=True)
    col_count = goal_piece.shape[0]
    pos_weight, neg_weight = pair_weights(pos_offset, neg_blocks, row_first, row_count, col_count)
    loss_sum, coeffs = score_terms(states, goal_piece, pos_weight, neg_weight)
    grad_rows = jnp.einsum("tqk,kte->qte", coeffs, goal_piece, preferred_element_type=jnp.float32)
    loss_sum, coeffs, grad_rows = (loss_sum, coeffs, grad_rows)
    folded = (grad_rows, loss_sum, coeffs)
    grad_states = folded[0]
    loss_sum = folded[1]
    coeff_all = folded[2]
    grad_goals = lax.psum_scatter(
        jnp.einsum("tqk,qte->kte", coeff_all, states, preferred_element_type=jnp.float32).astype(
            jnp.bfloat16
        ),
        "tm",
        scatter_dimension=0,
        tiled=True,
    ).astype(jnp.float32)
    loss_all = lax.psum(loss_sum, "tm")
    loss_mean = (loss_all / (traj_count * steps_all)).reshape(1)
    return (loss_mean, grad_states, grad_goals)


def solution(mesh):
    in_specs = (
        P("tm", "groups", None),
        P("tm", "groups", None),
        P("tm", "groups", None),
        P("tm", "groups", None),
    )
    out_specs = (P("groups"), P("tm", "groups", None), P("tm", "groups", None))
    return jax.shard_map(
        per_device, mesh=mesh, in_specs=in_specs, out_specs=out_specs, check_vma=False
    )
```

profile of v0, /device:TPU:0, one launch (start us, length us, event | category | flops | bytes accessed | tf_op | source)
XLA Modules:
  0.0 219.8 jit_solution(17836653208547374864)
XLA Ops:
  7.2 0.0 copy-start
  7.2 0.0 all-gather.2.cloned.1.call-start
  7.2 0.7 all-gather.2.cloned.1.call-update
  7.9 0.0 reduce-scatter.2.cloned.1.call-start
  8.0 0.7 add_bitcast_fusion
  8.7 0.1 convert_reduce_fusion.1
  8.8 0.8 convert_reduce_fusion
  9.6 77.6 %all-gather.2.cloned.1.call-done = bf16[4096,1,1024]{2,0,1:T(8,128)(2,1)} async-done(((bf16[256,1,1024]{2,0,1:T(8,128)(2,1)}), bf16[4096,1,1024]{2,0,1:T(8,128)(2,1)}) %all-gather.2.cloned.1.call-update) | async-done | bytes 8388624 | tf_op jit(solution)/shard_map/all_gather | solution.py:43
  87.2 0.0 copy-done
  87.2 11.5 %fusion.8 = (f32[]{:T(128)}, f32[256,4096]{1,0:T(8,128)S(1)}) fusion(f32[4096]{0:T(1024)S(1)} %convert_reduce_fusion, f32[4096]{0:T(1024)S(1)} %convert_reduce_fusion.1, s32[256]{0:T(256)S(1)} %iota_add_fusion, bf16[4096,1,1024]{2,0,1:T(8,128)(2,1)} %all-gather.2.cloned.1.call-done, bf16[256,1,1024]{2,0,1:T(8,128)(2,1)S(1)} %copy-done), kind=kOutput, calls=%fused_computation.11 | convolution fusion | flops 2168455168 | bytes 13140996 | tf_op jit(solution)/shard_map/qte,kte->tqk/dot_general | solution.py:30
  98.7 0.0 copy-start.1
  98.7 1.9 copy-done.1
  100.6 6.2 %convert_bitcast_fusion = bf16[4096,1,1024]{2,0,1:T(8,128)(2,1)} fusion(bf16[256,1,1024]{2,0,1:T(8,128)(2,1)S(1)} %copy-done, f32[256,4096]{1,0:T(8,128)S(1)} %get-tuple-element.10, f32[4096]{0:T(1024)S(1)} %convert_reduce_fusion, f32[4096]{0:T(1024)S(1)} %convert_reduce_fusion.1, s32[256]{0:T(256)S(1)} %iota_add_fusion), kind=kOutput, calls=%fused_computation.6 | convolution fusion | flops 2164260864 | bytes 13140992 | tf_op jit(solution)/shard_map/tqk,qte->kte/dot_general | solution.py:54
  106.8 0.0 reduce-scatter.2.cloned.1.call-update
  106.8 32.1 %psum.7 = f32[]{:T(128)} all-reduce(f32[]{:T(128)} %get-tuple-element.9), channel_id=1, replica_groups=mesh['groups'=2,'tm'=16] {'tm'}, use_global_device_ids=true, to_apply=%region_3.4 | all-reduce | flops 1 | bytes 8 | tf_op jit(solution)/shard_map/psum | solution.py:61
  138.9 8.2 %fusion.13 = f32[256,1,1024]{2,0,1:T(8,128)S(1)} fusion(bf16[4096,1,1024]{2,0,1:T(8,128)(2,1)} %all-gather.2.cloned.1.call-done, f32[256,4096]{1,0:T(8,128)} %copy-done.1, f32[4096]{0:T(1024)S(1)} %convert_reduce_fusion, f32[4096]{0:T(1024)S(1)} %convert_reduce_fusion.1, s32[256]{0:T(256)S(1)} %iota_add_fusion), kind=kOutput, calls=%fused_computation.18 | convolution fusion | flops 2160066560 | bytes 13665280 | tf_op jit(solution)/shard_map/tqk,kte->qte/dot_general | solution.py:47
  147.1 2.0 copy.9
  149.8 59.2 %reduce-scatter.2.cloned.1.call-done = bf16[256,1,1024]{2,0,1:T(8,128)(2,1)} async-done(((bf16[4096,1,1024]{2,0,1:T(8,128)(2,1)}), bf16[256,1,1024]{2,0,1:T(8,128)(2,1)}) %reduce-scatter.2.cloned.1.call-update) | async-done | bytes 524304 | tf_op jit(solution)/shard_map/reduce_scatter | solution.py:53
  209.0 2.8 %copy.10 = f32[256,1,1024]{2,1,0:T(1,128)} copy(bf16[256,1,1024]{2,0,1:T(8,128)(2,1)} %reduce-scatter.2.cloned.1.call-done) | data formatting | bytes 1572864
  (2 shorter events, 0.0 us)
Async XLA Ops:
  7.2 80.0 %copy-start = (bf16[256,1,1024]{2,0,1:T(8,128)(2,1)S(1)}, bf16[256,1,1024]{2,0,1:T(8,128)(2,1)}, u32[]{:S(2)}) copy-start(bf16[256,1,1024]{2,0,1:T(8,128)(2,1)} %param.4) | copy-start | bytes 1572868
  7.2 80.0 %all-gather.2.cloned.1.call-start = ((), (), s32[]{:S(2)}) async-start(), calls=%async_computation.1 | async-start | bytes 8912896 | tf_op jit(solution)/shard_map/all_gather | solution.py:43
  7.9 201.1 %reduce-scatter.2.cloned.1.call-start = ((), (), s32[]{:S(2)}) async-start(), calls=%async_computation.2 | async-start | bytes 8912896 | tf_op jit(solution)/shard_map/reduce_scatter | solution.py:53
  98.7 1.9 copy-start.1
Sparse Core Ops, SparseCore 0:
  10.2 77.0 all-gather.1
  107.0 102.0 reduce-scatter.1
where the time goes:
time: 220 us
  waiting for transfers between devices  138 us (63%)
  blocking collectives  32.1 us (15%)
  matrix products  25.9 us (12%)
  between operations  15.9 us (7%)
  local copies, waits for them, and re-layouts  6.8 us (3%)
    all_gather x1, waiting for transfers between devices, per_device(): goal_piece = lax.all_gather(goals, 'tm', axis=0, tiled=True)  77.6 us
    reduce_scatter x1, waiting for transfers between devices, per_device(): lax.psum_scatter(jnp.einsum('tqk,qte->kte', coeff_all, states, preferred_...  59.2 us
    psum x1, blocking collectives, per_device(): loss_all = lax.psum(loss_sum, 'tm')  32.1 us
    dot_general x1, matrix products, score_terms(): jnp.einsum('qte,kte->tqk', anchor_rows, goal_rows, preferred_element_type...  11.5 us
    dot_general x1, matrix products, per_device(): jnp.einsum('tqk,kte->qte', coeffs, goal_piece, preferred_element_type=jnp...  8.22 us
    unnamed x6, local copies, waits for them, and re-layouts  6.8 us
    dot_general x1, matrix products, per_device(): jnp.einsum('tqk,qte->kte', coeff_all, states, preferred_element_type=jnp....  6.2 us
  transfers between devices with their start and end apart: 2, of which 2 were waited for; matrix products, arithmetic and copies ran while one was open for 5% of the time, Pallas kernels for 0%

commit v1 on v0

v1 whole, which is shorter than its diff:
```python
import functools
import math

import jax
import jax.numpy as jnp
from jax import lax
from jax.experimental import pallas as pl
from jax.experimental.pallas import tpu as pltpu
from jax.sharding import PartitionSpec as P

AXIS = "tm"


def swap(value, bit, size):
    return lax.ppermute(value, AXIS, [(i, i ^ bit) for i in range(size)])


def subsets(bits):
    found = [0]
    for bit in bits:
        found = found + [offset ^ bit for offset in found]
    return found


def tile_kernel(row_xors, col_xors, own_ref, *refs):
    n_row, n_col = len(row_xors), len(col_xors)
    pos_refs, refs = refs[:n_row], refs[n_row:]
    neg_refs, refs = refs[:n_row], refs[n_row:]
    row_hbm, refs = refs[:n_row], refs[n_row:]
    col_hbm, refs = refs[:n_col], refs[n_col:]
    loss_ref, refs = refs[0], refs[1:]
    row_out, refs = refs[:n_row], refs[n_row:]
    col_out, refs = refs[:n_col], refs[n_col:]
    rows, cols, coeff, row_grad, col_grad, in_sem, out_sem = refs
    length, width = row_hbm[0].shape
    inv_root = 1.0 / math.sqrt(width)
    own = own_ref[0]

    loads = []
    for i in range(n_row):
        loads.append(pltpu.make_async_copy(row_hbm[i], rows.at[pl.ds(i * length, length)], in_sem.at[i]))
    for j in range(n_col):
        loads.append(pltpu.make_async_copy(col_hbm[j], cols.at[pl.ds(j * length, length)], in_sem.at[n_row + j]))
    for load in loads:
        load.start()

    weights = []
    for i in range(n_row):
        block = own ^ row_xors[i]
        line = []
        for j in range(n_col):
            target = own ^ col_xors[j]
            pos = jnp.int32(0)
            for p in range(pos_refs[i].shape[0]):
                pos = pos + jnp.where(pos_refs[i][p] + block == target, 1, 0)
            neg = jnp.int32(0)
            for k in range(neg_refs[i].shape[0]):
                neg = neg + jnp.where(neg_refs[i][k] == target, 1, 0)
            line.append((pos.astype(jnp.float32), neg.astype(jnp.float32)))
        weights.append(line)

    for load in loads:
        load.wait()

    later = lax.broadcasted_iota(jnp.int32, (length, length), 1) > lax.broadcasted_iota(
        jnp.int32, (length, length), 0
    )
    loss = jnp.zeros((8, length), jnp.float32)
    for i in range(n_row):
        row_slice = pl.ds(i * length, length)
        for j in range(n_col):
            col_slice = pl.ds(j * length, length)
            scores = (
                lax.dot_general(
                    rows[row_slice, :], cols[col_slice, :], (((1,), (1,)), ((), ())),
                    preferred_element_type=jnp.float32,
                )
                * inv_root
            )
            pos, neg = weights[i][j]
            decay = jnp.exp(-jnp.abs(scores))
            whole = 1.0 + decay
            large = 1.0 / whole
            small = decay * large
            up = scores >= 0.0
            rise = jnp.where(up, large, small)
            fall = jnp.where(up, small, large)
            above = jnp.maximum(scores, 0.0)
            below = above - scores
            if row_xors[i] == col_xors[j]:
                pos_tile = jnp.where(later, pos, 0.0)
                soft = jnp.log(whole)
                part = pos_tile * (below + soft) + neg * (above + soft)
                coeffs = (neg * rise - pos_tile * fall) * inv_root
                while part.shape[0] > 8:
                    half = part.shape[0] // 2
                    part = part[:half] + part[half:]
            else:
                coeffs = (neg * inv_root) * rise - (pos * inv_root) * fall
                part = neg * above + pos * below
                while part.shape[0] > 8:
                    half = part.shape[0] // 2
                    part = part[:half] + part[half:]
                    whole = whole[:half] * whole[half:]
                part = part + (pos + neg) * jnp.log(whole)
            loss = loss + part
            coeff[row_slice, col_slice] = coeffs.astype(jnp.bfloat16)
        row_grad[row_slice, :] = jnp.dot(
            coeff[row_slice, :], cols[...], preferred_element_type=jnp.float32
        ).astype(row_grad.dtype)
        pltpu.make_async_copy(row_grad.at[row_slice], row_out[i], out_sem.at[i]).start()
    for j in range(n_col):
        col_slice = pl.ds(j * length, length)
        col_grad[col_slice, :] = lax.dot_general(
            coeff[:, col_slice], rows[...], (((0,), (0,)), ((), ())), preferred_element_type=jnp.float32
        ).astype(col_grad.dtype)
        pltpu.make_async_copy(col_grad.at[col_slice], col_out[j], out_sem.at[n_row + j]).start()
    loss_ref[0] = jnp.sum(loss)
    for i in range(n_row):
        pltpu.make_async_copy(row_grad.at[pl.ds(i * length, length)], row_out[i], out_sem.at[i]).wait()
    for j in range(n_col):
        pltpu.make_async_copy(
            col_grad.at[pl.ds(j * length, length)], col_out[j], out_sem.at[n_row + j]
        ).wait()


def tiles(own, pos, neg, rows, cols, row_xors, col_xors):
    n_row, n_col = len(rows), len(cols)
    length, width = rows[0].shape
    smem = pl.BlockSpec(memory_space=pltpu.SMEM)
    anywhere = pl.BlockSpec(memory_space=pl.ANY)
    block = jax.ShapeDtypeStruct((length, width), jnp.float32)
    flops = 6 * n_row * n_col * length * length * width
    return pl.pallas_call(
        functools.partial(tile_kernel, row_xors, col_xors),
        in_specs=[smem] * (1 + 2 * n_row) + [anywhere] * (n_row + n_col),
        out_specs=[smem] + [anywhere] * (n_row + n_col),
        out_shape=[jax.ShapeDtypeStruct((1,), jnp.float32)] + [block] * (n_row + n_col),
        scratch_shapes=[
            pltpu.VMEM((n_row * length, width), jnp.bfloat16),
            pltpu.VMEM((n_col * length, width), jnp.bfloat16),
            pltpu.VMEM((n_row * length, n_col * length), jnp.bfloat16),
            pltpu.VMEM((n_row * length, width), jnp.float32),
            pltpu.VMEM((n_col * length, width), jnp.float32),
            pltpu.SemaphoreType.DMA((n_row + n_col,)),
            pltpu.SemaphoreType.DMA((n_row + n_col,)),
        ],
        cost_estimate=pl.CostEstimate(
            flops=flops, bytes_accessed=6 * (n_row + n_col) * length * width,
            transcendentals=3 * n_row * n_col * length * length,
        ),
        compiler_params=pltpu.CompilerParams(vmem_limit_bytes=48 << 20),
        name="tiles",
    )(own, *pos, *neg, *rows, *cols)


def per_device(states, goals, pos_offset, neg_blocks):
    size = lax.axis_size(AXIS)
    length, width = states.shape[0], states.shape[2]
    high = size // 2
    inner = []
    bit = size // 4
    while bit > 1:
        inner.append(bit)
        bit //= 2
    row_xors, col_xors = [0, 1, high, high ^ 1], subsets(inner)
    state, goal = states.reshape(length, width), goals.reshape(length, width)
    table = jnp.concatenate([pos_offset.reshape(-1), neg_blocks.reshape(-1)])
    n_pos = pos_offset.size

    pair = swap(state, high, size)
    cols = [goal]
    for bit in inner:
        cols = cols + [swap(c, bit, size) for c in cols]
    pair_table = swap(table, high, size)
    rows = [state, swap(state, 1, size), pair, swap(pair, 1, size)]
    tables = [table, swap(table, 1, size), pair_table, swap(pair_table, 1, size)]
    own = lax.axis_index(AXIS).astype(jnp.int32).reshape(1)
    outs = tiles(
        own, [t[:n_pos] for t in tables], [t[n_pos:] for t in tables], rows, cols, row_xors, col_xors
    )
    loss, row_parts, col_parts = outs[0], outs[1:5], outs[5:]

    here = row_parts[0] + swap(row_parts[1].astype(jnp.bfloat16), 1, size)
    there = row_parts[2] + swap(row_parts[3].astype(jnp.bfloat16), 1, size)
    grad_states = here + swap(there.astype(jnp.bfloat16), high, size)

    parts = dict(zip(col_xors, col_parts))
    for bit in reversed(inner):
        moved = {k: swap(v.astype(jnp.bfloat16), bit, size) for k, v in parts.items() if k & bit}
        parts = {k: v + moved[k ^ bit].astype(jnp.float32) for k, v in parts.items() if not k & bit}
    grad_goals = parts[0]

    bit = 1
    while bit < size:
        loss = loss + swap(loss, bit, size)
        bit *= 2
    loss_mean = loss / (size * length)
    return (
        loss_mean,
        grad_states.reshape(length, 1, width),
        grad_goals.reshape(length, 1, width),
    )


def solution(mesh):
    spec = P("tm", "groups", None)
    return jax.shard_map(
        per_device,
        mesh=mesh,
        in_specs=(spec,) * 4,
        out_specs=(P("groups"), spec, spec),
        check_vma=False,
    )
```

time: 220 us -> 109 us (0.50)
  waiting for transfers between devices: 138 us -> 46.3 us
  starting transfers between devices: 0.08 us -> 34.8 us
  blocking collectives: 32.1 us -> 0 us
  matrix products: 25.9 us -> 0 us
  Pallas kernels: 0 us -> 13.3 us
  between operations: 15.9 us -> 4.83 us
    all_gather x1 -> x0, waiting for transfers between devices: 77.6 us -> none  [per_device(): goal_piece = lax.all_gather(goals, 'tm', axis=0, tiled=True)]
    reduce_scatter x1 -> x0, waiting for transfers between devices: 59.2 us -> none  [per_device(): lax.psum_scatter(jnp.einsum('tqk,qte->kte', coeff_all, states, preferred_...]
    ppermute x0 -> x19, waiting for transfers between devices: none -> 46.3 us  [swap(): return lax.ppermute(value, AXIS, [(i, i ^ bit) for i in range(size)])]
    ppermute x0 -> x19, starting transfers between devices: none -> 34.8 us  [swap(): return lax.ppermute(value, AXIS, [(i, i ^ bit) for i in range(size)])]
    psum x1 -> x0, blocking collectives: 32.1 us -> none  [per_device(): loss_all = lax.psum(loss_sum, 'tm')]
    dot_general x3 -> x0, matrix products: 25.9 us -> none  [the longest x1 11.5 us: score_terms(): jnp.einsum('qte,kte->tqk', anchor_rows, goal_rows, preferred_element_type...]
    pallas_call x0 -> x1, Pallas kernels: none -> 13.3 us  [tiles(): pl.pallas_call(functools.partial(tile_kernel, row_xors, col_xors), in_spe...]
    unnamed x6 -> x22, local copies, waits for them, and re-layouts: 6.8 us -> 7.34 us
  transfers between devices with their start and end apart: 2 -> 19, of which waited for: 2 -> 10; matrix products, arithmetic and copies ran while one was open for 5% -> 3% of each run, Pallas kernels for 0% -> 0%
where the time goes in v1:
time: 109 us
  waiting for transfers between devices  46.3 us (42%)
  starting transfers between devices  34.8 us (32%)
  Pallas kernels  13.3 us (12%)
  local copies, waits for them, and re-layouts  7.56 us (7%)
  between operations  4.83 us (4%)
  other arithmetic  2.41 us (2%)
    ppermute x19, waiting for transfers between devices, swap(): return lax.ppermute(value, AXIS, [(i, i ^ bit) for i in range(size)])  46.3 us
    ppermute x19, starting transfers between devices, swap(): return lax.ppermute(value, AXIS, [(i, i ^ bit) for i in range(size)])  34.8 us
    pallas_call x1, Pallas kernels, tiles(): pl.pallas_call(functools.partial(tile_kernel, row_xors, col_xors), in_spe...  13.3 us
    unnamed x22, local copies, waits for them, and re-layouts  7.34 us
  transfers between devices with their start and end apart: 19, of which 10 were waited for; matrix products, arithmetic and copies ran while one was open for 3% of the time, Pallas kernels for 0%

profile of v1, /device:TPU:0, one launch (start us, length us, event | category | flops | bytes accessed | tf_op | source)
XLA Modules:
  0.0 109.2 jit_solution(16494345992509400922)
XLA Ops:
  0.6 4.1 %collective-permute-start.4 = (bf16[256,1024]{1,0:T(8,128)(2,1)}, bf16[256,1024]{1,0:T(8,128)(2,1)S(1)}, u32[]{:S(2)}, u32[]{:S(2)}) collective-permute-start(bf16[256,1024]{1,0:T(8,128)(2,1)} %bitcast.12), channel_id=1, source_target_pairs={{0,8},{1,9},{2,10},{3,11},{4,12},{5,13},{6,14},{7,15},{8,0},{9,1},... | collective-permute-start | bytes 1572872 | tf_op jit(solution)/shard_map/ppermute | solution.py:15
  4.8 1.6 %collective-permute-start.6 = (bf16[256,1024]{1,0:T(8,128)(2,1)}, bf16[256,1024]{1,0:T(8,128)(2,1)S(1)}, u32[]{:S(2)}, u32[]{:S(2)}) collective-permute-start(bf16[256,1024]{1,0:T(8,128)(2,1)} %bitcast.15), channel_id=1, source_target_pairs={{0,4},{1,5},{2,6},{3,7},{4,0},{5,1},{6,2},{7,3},{8,12},{9,13},{10,... | collective-permute-start | bytes 1572872 | tf_op jit(solution)/shard_map/ppermute | solution.py:15
  6.3 1.5 %collective-permute-start.7 = (bf16[256,1024]{1,0:T(8,128)(2,1)}, bf16[256,1024]{1,0:T(8,128)(2,1)S(1)}, u32[]{:S(2)}, u32[]{:S(2)}) collective-permute-start(bf16[256,1024]{1,0:T(8,128)(2,1)} %bitcast.16), channel_id=1, source_target_pairs={{0,2},{1,3},{2,0},{3,1},{4,6},{5,7},{6,4},{7,5},{8,10},{9,11},{10,... | collective-permute-start | bytes 1572872 | tf_op jit(solution)/shard_map/ppermute | solution.py:15
  7.9 20.4 %collective-permute-done.4.refs_10_ = bf16[256,1024]{1,0:T(8,128)(2,1)S(1)} collective-permute-done((bf16[256,1024]{1,0:T(8,128)(2,1)}, bf16[256,1024]{1,0:T(8,128)(2,1)S(1)}, u32[]{:S(2)}, u32[]{:S(2)}) %collective-permute-start.4) | collective-permute-done | bytes 524320 | tf_op jit(solution)/shard_map/ppermute | solution.py:15
  28.2 0.2 collective-permute-done.6.refs_13_
  28.4 1.6 %collective-permute-start.8 = (bf16[256,1024]{1,0:T(8,128)(2,1)S(1)}, bf16[256,1024]{1,0:T(8,128)(2,1)S(1)}, u32[]{:S(2)}, u32[]{:S(2)}) collective-permute-start(bf16[256,1024]{1,0:T(8,128)(2,1)S(1)} %collective-permute-done.6.refs_13_), channel_id=1, source_target_pairs={{0,2},{1,3},{2,0},{3,1},{4,6},{5,7},{6,4},{7,5},{8,10},{9,11},{10,... | collective-permute-start | bytes 1572872 | tf_op jit(solution)/shard_map/ppermute | solution.py:15
  30.0 0.7 copy-done.2
  30.7 0.0 copy-done.3
  30.7 0.1 pad_add_fusion
  30.7 1.3 %collective-permute-start.1 = (s32[24]{0:T(128)S(1)}, s32[24]{0:T(128)S(1)}, u32[]{:S(2)}, u32[]{:S(2)}) collective-permute-start(s32[24]{0:T(128)S(1)} %pad_add_fusion), channel_id=1, source_target_pairs={{0,8},{1,9},{2,10},{3,11},{4,12},{5,13},{6,14},{7,15},{8,0},{9,1},... | collective-permute-start | bytes 296 | tf_op jit(solution)/shard_map/ppermute | solution.py:15
  32.1 3.1 %collective-permute-done.1 = s32[24]{0:T(128)S(1)} collective-permute-done((s32[24]{0:T(128)S(1)}, s32[24]{0:T(128)S(1)}, u32[]{:S(2)}, u32[]{:S(2)}) %collective-permute-start.1) | collective-permute-done | bytes 128 | tf_op jit(solution)/shard_map/ppermute | solution.py:15
  35.2 0.1 slice.22.refs_6_
  35.3 1.1 collective-permute-done
  36.4 0.2 collective-permute-start.2
  36.5 0.1 slice.21.refs_5_
  36.6 0.9 collective-permute-done.2
  37.5 0.1 slice.23.refs_7_
  37.6 5.0 %collective-permute-done.8.refs_15_ = bf16[256,1024]{1,0:T(8,128)(2,1)S(1)} collective-permute-done((bf16[256,1024]{1,0:T(8,128)(2,1)S(1)}, bf16[256,1024]{1,0:T(8,128)(2,1)S(1)}, u32[]{:S(2)}, u32[]{:S(2)}) %collective-permute-start.8) | collective-permute-done | bytes 524320 | tf_op jit(solution)/shard_map/ppermute | solution.py:15
  42.6 1.0 copy-done
  43.6 1.0 copy-done.1
  44.7 13.3 %tiles.1 = (f32[1]{0:T(128)}, f32[256,1024]{1,0:T(8,128)S(1)}, f32[256,1024]{1,0:T(8,128)}, f32[256,1024]{1,0:T(8,128)}, f32[256,1024]{1,0:T(8,128)}, /*index=5*...) custom-call(s32[1]{0:T(128)} %bitcast.own_ref, s32[8]{0:T(128)S(1)} %bitcast.19, ...), custom_call_target="tpu_custom_call" | custom-call | flops 6442450944 | bytes 12582912 | tf_op jit(solution)/shard_map/tiles/pallas_call | solution.py:134
  58.0 1.4 %convert_element_type.44 = bf16[256,1024]{1,0:T(8,128)(2,1)S(1)} convert(f32[256,1024]{1,0:T(8,128)} %get-tuple-element.20) | non-fusion elementwise | flops 262144 | bytes 1572864 | tf_op jit(solution)/shard_map/convert_element_type | solution.py:190
  59.4 1.6 %collective-permute-start.17 = (bf16[256,1024]{1,0:T(8,128)(2,1)S(1)}, bf16[256,1024]{1,0:T(8,128)(2,1)S(1)}, u32[]{:S(2)}, u32[]{:S(2)}) collective-permute-start(bf16[256,1024]{1,0:T(8,128)(2,1)S(1)} %convert_element_type.44), channel_id=1, source_target_pairs={{0,2},{1,3},{2,0},{3,1},{4,6},{5,7},{6,4},{7,5},{8,10},{9,11},{10,... | collective-permute-start | bytes 1572872 | tf_op jit(solution)/shard_map/ppermute | solution.py:15
  61.0 0.1 convert_element_type.38
  61.1 0.1 collective-permute-start.14
  61.2 0.1 convert_element_type.42
  61.2 1.1 collective-permute-start.16
  62.3 11.9 %collective-permute-done.17 = bf16[256,1024]{1,0:T(8,128)(2,1)S(1)} collective-permute-done((bf16[256,1024]{1,0:T(8,128)(2,1)S(1)}, bf16[256,1024]{1,0:T(8,128)(2,1)S(1)}, u32[]{:S(2)}, u32[]{:S(2)}) %collective-permute-start.17) | collective-permute-done | bytes 524320 | tf_op jit(solution)/shard_map/ppermute | solution.py:15
  74.2 0.1 add_convert_fusion
  74.4 0.0 copy-start.8
  74.4 0.8 collective-permute-start.18
  75.2 0.3 copy-done.5
  75.5 0.1 convert_element_type.36
  75.5 0.1 collective-permute-start.13
  75.6 0.2 copy-done.8
  75.8 0.2 add_convert_fusion.1
  76.0 2.9 %collective-permute-start.15 = (bf16[256,1024]{1,0:T(8,128)(2,1)S(1)}, bf16[256,1024]{1,0:T(8,128)(2,1)S(1)}, u32[]{:S(2)}, u32[]{:S(2)}) collective-permute-start(bf16[256,1024]{1,0:T(8,128)(2,1)S(1)} %add_convert_fusion.1), channel_id=1, source_target_pairs={{0,8},{1,9},{2,10},{3,11},{4,12},{5,13},{6,14},{7,15},{8,0},{9,1},... | collective-permute-start | bytes 1572872 | tf_op jit(solution)/shard_map/ppermute | solution.py:15
  78.9 0.2 collective-permute-start.9
  79.1 1.3 %collective-permute-done.9 = f32[1]{0:T(128)} collective-permute-done((f32[1]{0:T(128)}, f32[1]{0:T(128)}, u32[]{:S(2)}, u32[]{:S(2)}) %collective-permute-start.9) | collective-permute-done | bytes 36 | tf_op jit(solution)/shard_map/ppermute | solution.py:15
  81.6 2.9 %collective-permute-start.10 = (f32[1]{0:T(128)}, f32[1]{0:T(128)}, u32[]{:S(2)}, u32[]{:S(2)}) collective-permute-start(f32[1]{0:T(128)} %add.30), channel_id=1, source_target_pairs={{0,2},{1,3},{2,0},{3,1},{4,6},{5,7},{6,4},{7,5},{8,10},{9,11},{10,... | collective-permute-start | bytes 20 | tf_op jit(solution)/shard_map/ppermute | solution.py:15
  84.4 0.9 collective-permute-done.10
  85.9 8.7 %collective-permute-start.11 = (f32[1]{0:T(128)}, f32[1]{0:T(128)}, u32[]{:S(2)}, u32[]{:S(2)}) collective-permute-start(f32[1]{0:T(128)} %add.31), channel_id=1, source_target_pairs={{0,4},{1,5},{2,6},{3,7},{4,0},{5,1},{6,2},{7,3},{8,12},{9,13},{10,... | collective-permute-start | bytes 20 | tf_op jit(solution)/shard_map/ppermute | solution.py:15
  95.1 6.2 %collective-permute-start.12 = (f32[1]{0:T(128)}, f32[1]{0:T(128)}, u32[]{:S(2)}, u32[]{:S(2)}) collective-permute-start(f32[1]{0:T(128)} %add.32), channel_id=1, source_target_pairs={{0,8},{1,9},{2,10},{3,11},{4,12},{5,13},{6,14},{7,15},{8,0},{9,1},... | collective-permute-start | bytes 20 | tf_op jit(solution)/shard_map/ppermute | solution.py:15
  101.3 1.5 %collective-permute-done.12 = f32[1]{0:T(128)} collective-permute-done((f32[1]{0:T(128)}, f32[1]{0:T(128)}, u32[]{:S(2)}, u32[]{:S(2)}) %collective-permute-start.12) | collective-permute-done | bytes 36 | tf_op jit(solution)/shard_map/ppermute | solution.py:15
  103.5 0.2 add_bitcast_fusion
  103.7 2.0 %copy.8 = f32[256,1,1024]{2,1,0:T(1,128)} copy(f32[256,1,1024]{2,0,1:T(8,128)S(1)} %add_bitcast_fusion) | data formatting | bytes 2097152
  105.7 0.2 add_bitcast_fusion.1
  106.0 2.1 %copy.7 = f32[256,1,1024]{2,1,0:T(1,128)} copy(f32[256,1,1024]{2,0,1:T(8,128)S(1)} %add_bitcast_fusion.1) | data formatting | bytes 2097152
  (25 shorter events, 0.1 us)
Async XLA Ops:
  0.6 27.6 %collective-permute-start.4 = (bf16[256,1024]{1,0:T(8,128)(2,1)}, bf16[256,1024]{1,0:T(8,128)(2,1)S(1)}, u32[]{:S(2)}, u32[]{:S(2)}) collective-permute-start(bf16[256,1024]{1,0:T(8,128)(2,1)} %bitcast.12), channel_id=1, source_target_pairs={{0,8},{1,9},{2,10},{3,11},{4,12},{5,13},{6,14},{7,15},{8,0},{9,1},... | collective-permute-start | bytes 1572872 | tf_op jit(solution)/shard_map/ppermute | solution.py:15
  4.8 23.7 %collective-permute-start.6 = (bf16[256,1024]{1,0:T(8,128)(2,1)}, bf16[256,1024]{1,0:T(8,128)(2,1)S(1)}, u32[]{:S(2)}, u32[]{:S(2)}) collective-permute-start(bf16[256,1024]{1,0:T(8,128)(2,1)} %bitcast.15), channel_id=1, source_target_pairs={{0,4},{1,5},{2,6},{3,7},{4,0},{5,1},{6,2},{7,3},{8,12},{9,13},{10,... | collective-permute-start | bytes 1572872 | tf_op jit(solution)/shard_map/ppermute | solution.py:15
  6.3 31.3 %collective-permute-start.3 = (bf16[256,1024]{1,0:T(8,128)(2,1)}, bf16[256,1024]{1,0:T(8,128)(2,1)S(1)}, u32[]{:S(2)}, u32[]{:S(2)}) collective-permute-start(bf16[256,1024]{1,0:T(8,128)(2,1)} %bitcast.13), channel_id=1, source_target_pairs={{0,1},{1,0},{2,3},{3,2},{4,5},{5,4},{6,7},{7,6},{8,9},{9,8},{10,11... | collective-permute-start | bytes 1572872 | tf_op jit(solution)/shard_map/ppermute | solution.py:15
  6.3 31.3 %collective-permute-start.7 = (bf16[256,1024]{1,0:T(8,128)(2,1)}, bf16[256,1024]{1,0:T(8,128)(2,1)S(1)}, u32[]{:S(2)}, u32[]{:S(2)}) collective-permute-start(bf16[256,1024]{1,0:T(8,128)(2,1)} %bitcast.16), channel_id=1, source_target_pairs={{0,2},{1,3},{2,0},{3,1},{4,6},{5,7},{6,4},{7,5},{8,10},{9,11},{10,... | collective-permute-start | bytes 1572872 | tf_op jit(solution)/shard_map/ppermute | solution.py:15
  28.2 9.4 %collective-permute-start.5 = (bf16[256,1024]{1,0:T(8,128)(2,1)S(1)}, bf16[256,1024]{1,0:T(8,128)(2,1)S(1)}, u32[]{:S(2)}, u32[]{:S(2)}) collective-permute-start(bf16[256,1024]{1,0:T(8,128)(2,1)S(1)} %collective-permute-done.4.refs_10_), channel_id=1, source_target_pairs={{0,1},{1,0},{2,3},{3,2},{4,5},{5,4},{6,7},{7,6},{8,9},{9,8},{10,11... | collective-permute-start | bytes 1572872 | tf_op jit(solution)/shard_map/ppermute | solution.py:15
  28.4 14.2 %collective-permute-start.8 = (bf16[256,1024]{1,0:T(8,128)(2,1)S(1)}, bf16[256,1024]{1,0:T(8,128)(2,1)S(1)}, u32[]{:S(2)}, u32[]{:S(2)}) collective-permute-start(bf16[256,1024]{1,0:T(8,128)(2,1)S(1)} %collective-permute-done.6.refs_13_), channel_id=1, source_target_pairs={{0,2},{1,3},{2,0},{3,1},{4,6},{5,7},{6,4},{7,5},{8,10},{9,11},{10,... | collective-permute-start | bytes 1572872 | tf_op jit(solution)/shard_map/ppermute | solution.py:15
  30.0 0.7 copy-start.2
  30.0 0.7 copy-start.3
  30.7 4.5 %collective-permute-start.1 = (s32[24]{0:T(128)S(1)}, s32[24]{0:T(128)S(1)}, u32[]{:S(2)}, u32[]{:S(2)}) collective-permute-start(s32[24]{0:T(128)S(1)} %pad_add_fusion), channel_id=1, source_target_pairs={{0,8},{1,9},{2,10},{3,11},{4,12},{5,13},{6,14},{7,15},{8,0},{9,1},... | collective-permute-start | bytes 296 | tf_op jit(solution)/shard_map/ppermute | solution.py:15
  35.2 1.2 %collective-permute-start = (s32[24]{0:T(128)S(1)}, s32[24]{0:T(128)S(1)}, u32[]{:S(2)}, u32[]{:S(2)}) collective-permute-start(s32[24]{0:T(128)S(1)} %pad_add_fusion), channel_id=1, source_target_pairs={{0,1},{1,0},{2,3},{3,2},{4,5},{5,4},{6,7},{7,6},{8,9},{9,8},{10,11... | collective-permute-start | bytes 296 | tf_op jit(solution)/shard_map/ppermute | solution.py:15
  36.4 1.2 %collective-permute-start.2 = (s32[24]{0:T(128)S(1)}, s32[24]{0:T(128)S(1)}, u32[]{:S(2)}, u32[]{:S(2)}) collective-permute-start(s32[24]{0:T(128)S(1)} %collective-permute-done.1), channel_id=1, source_target_pairs={{0,1},{1,0},{2,3},{3,2},{4,5},{5,4},{6,7},{7,6},{8,9},{9,8},{10,11... | collective-permute-start | bytes 296 | tf_op jit(solution)/shard_map/ppermute | solution.py:15
  42.6 1.0 copy-start
  43.6 1.0 copy-start.1
  58.0 3.0 %copy-start.7 = (f32[256,1024]{1,0:T(8,128)S(1)}, f32[256,1024]{1,0:T(8,128)}, u32[]{:S(2)}) copy-start(f32[256,1024]{1,0:T(8,128)} %get-tuple-element.16) | copy-start | bytes 3145732
  59.4 1.8 %copy-start.6 = (f32[256,1024]{1,0:T(8,128)S(1)}, f32[256,1024]{1,0:T(8,128)}, u32[]{:S(2)}) copy-start(f32[256,1024]{1,0:T(8,128)} %get-tuple-element.18) | copy-start | bytes 3145732
  59.4 14.9 %collective-permute-start.17 = (bf16[256,1024]{1,0:T(8,128)(2,1)S(1)}, bf16[256,1024]{1,0:T(8,128)(2,1)S(1)}, u32[]{:S(2)}, u32[]{:S(2)}) collective-permute-start(bf16[256,1024]{1,0:T(8,128)(2,1)S(1)} %convert_element_type.44), channel_id=1, source_target_pairs={{0,2},{1,3},{2,0},{3,1},{4,6},{5,7},{6,4},{7,5},{8,10},{9,11},{10,... | collective-permute-start | bytes 1572872 | tf_op jit(solution)/shard_map/ppermute | solution.py:15
  61.1 13.2 %copy-start.9 = (f32[256,1024]{1,0:T(8,128)S(1)}, f32[256,1024]{1,0:T(8,128)}, u32[]{:S(2)}) copy-start(f32[256,1024]{1,0:T(8,128)} %get-tuple-element.19) | copy-start | bytes 3145732
  61.1 14.5 %collective-permute-start.14 = (bf16[256,1024]{1,0:T(8,128)(2,1)S(1)}, bf16[256,1024]{1,0:T(8,128)(2,1)S(1)}, u32[]{:S(2)}, u32[]{:S(2)}) collective-permute-start(bf16[256,1024]{1,0:T(8,128)(2,1)S(1)} %convert_element_type.38), channel_id=1, source_target_pairs={{0,1},{1,0},{2,3},{3,2},{4,5},{5,4},{6,7},{7,6},{8,9},{9,8},{10,11... | collective-permute-start | bytes 1572872 | tf_op jit(solution)/shard_map/ppermute | solution.py:15
  61.2 42.2 %collective-permute-start.16 = (bf16[256,1024]{1,0:T(8,128)(2,1)S(1)}, bf16[256,1024]{1,0:T(8,128)(2,1)S(1)}, u32[]{:S(2)}, u32[]{:S(2)}) collective-permute-start(bf16[256,1024]{1,0:T(8,128)(2,1)S(1)} %convert_element_type.42), channel_id=1, source_target_pairs={{0,2},{1,3},{2,0},{3,1},{4,6},{5,7},{6,4},{7,5},{8,10},{9,11},{10,... | collective-permute-start | bytes 1572872 | tf_op jit(solution)/shard_map/ppermute | solution.py:15
  74.2 1.2 %copy-start.5 = (f32[256,1024]{1,0:T(8,128)S(1)}, f32[256,1024]{1,0:T(8,128)}, u32[]{:S(2)}) copy-start(f32[256,1024]{1,0:T(8,128)} %get-tuple-element.14) | copy-start | bytes 3145732
  74.4 1.4 %copy-start.8 = (f32[256,1024]{1,0:T(8,128)S(1)}, f32[256,1024]{1,0:T(8,128)}, u32[]{:S(2)}) copy-start(f32[256,1024]{1,0:T(8,128)} %get-tuple-element.15) | copy-start | bytes 3145732
  74.4 29.0 %collective-permute-start.18 = (bf16[256,1024]{1,0:T(8,128)(2,1)S(1)}, bf16[256,1024]{1,0:T(8,128)(2,1)S(1)}, u32[]{:S(2)}, u32[]{:S(2)}) collective-permute-start(bf16[256,1024]{1,0:T(8,128)(2,1)S(1)} %add_convert_fusion), channel_id=1, source_target_pairs={{0,4},{1,5},{2,6},{3,7},{4,0},{5,1},{6,2},{7,3},{8,12},{9,13},{10,... | collective-permute-start | bytes 1572872 | tf_op jit(solution)/shard_map/ppermute | solution.py:15
  75.5 30.2 %collective-permute-start.13 = (bf16[256,1024]{1,0:T(8,128)(2,1)S(1)}, bf16[256,1024]{1,0:T(8,128)(2,1)S(1)}, u32[]{:S(2)}, u32[]{:S(2)}) collective-permute-start(bf16[256,1024]{1,0:T(8,128)(2,1)S(1)} %convert_element_type.36), channel_id=1, source_target_pairs={{0,1},{1,0},{2,3},{3,2},{4,5},{5,4},{6,7},{7,6},{8,9},{9,8},{10,11... | collective-permute-start | bytes 1572872 | tf_op jit(solution)/shard_map/ppermute | solution.py:15
  75.8 27.6 %copy-start.4 = (f32[256,1024]{1,0:T(8,128)S(1)}, f32[256,1024]{1,0:T(8,128)}, u32[]{:S(2)}) copy-start(f32[256,1024]{1,0:T(8,128)} %get-tuple-element.17) | copy-start | bytes 3145732
  76.0 29.7 %collective-permute-start.15 = (bf16[256,1024]{1,0:T(8,128)(2,1)S(1)}, bf16[256,1024]{1,0:T(8,128)(2,1)S(1)}, u32[]{:S(2)}, u32[]{:S(2)}) collective-permute-start(bf16[256,1024]{1,0:T(8,128)(2,1)S(1)} %add_convert_fusion.1), channel_id=1, source_target_pairs={{0,8},{1,9},{2,10},{3,11},{4,12},{5,13},{6,14},{7,15},{8,0},{9,1},... | collective-permute-start | bytes 1572872 | tf_op jit(solution)/shard_map/ppermute | solution.py:15
  78.9 1.5 %collective-permute-start.9 = (f32[1]{0:T(128)}, f32[1]{0:T(128)}, u32[]{:S(2)}, u32[]{:S(2)}) collective-permute-start(f32[1]{0:T(128)} %get-tuple-element.12), channel_id=1, source_target_pairs={{0,1},{1,0},{2,3},{3,2},{4,5},{5,4},{6,7},{7,6},{8,9},{9,8},{10,11... | collective-permute-start | bytes 20 | tf_op jit(solution)/shard_map/ppermute | solution.py:15
  81.6 3.7 %collective-permute-start.10 = (f32[1]{0:T(128)}, f32[1]{0:T(128)}, u32[]{:S(2)}, u32[]{:S(2)}) collective-permute-start(f32[1]{0:T(128)} %add.30), channel_id=1, source_target_pairs={{0,2},{1,3},{2,0},{3,1},{4,6},{5,7},{6,4},{7,5},{8,10},{9,11},{10,... | collective-permute-start | bytes 20 | tf_op jit(solution)/shard_map/ppermute | solution.py:15
  85.9 8.7 %collective-permute-start.11 = (f32[1]{0:T(128)}, f32[1]{0:T(128)}, u32[]{:S(2)}, u32[]{:S(2)}) collective-permute-start(f32[1]{0:T(128)} %add.31), channel_id=1, source_target_pairs={{0,4},{1,5},{2,6},{3,7},{4,0},{5,1},{6,2},{7,3},{8,12},{9,13},{10,... | collective-permute-start | bytes 20 | tf_op jit(solution)/shard_map/ppermute | solution.py:15
  95.1 7.8 %collective-permute-start.12 = (f32[1]{0:T(128)}, f32[1]{0:T(128)}, u32[]{:S(2)}, u32[]{:S(2)}) collective-permute-start(f32[1]{0:T(128)} %add.32), channel_id=1, source_target_pairs={{0,8},{1,9},{2,10},{3,11},{4,12},{5,13},{6,14},{7,15},{8,0},{9,1},... | collective-permute-start | bytes 20 | tf_op jit(solution)/shard_map/ppermute | solution.py:15

commit v2 on v0

v2 whole, which is shorter than its diff:
```python
import functools
import math

import jax
import jax.numpy as jnp
from jax import lax
from jax.experimental import pallas as pl
from jax.experimental.pallas import tpu as pltpu
from jax.sharding import PartitionSpec as P


AXIS = "tm"


def swap(value, offset, size, only=lambda i: True):
    return lax.ppermute(value, AXIS, [(i, i ^ offset) for i in range(size) if only(i)])


def subsets(bits):
    found = [0]
    for bit in bits:
        found = found + [offset ^ bit for offset in found]
    return found


def fold(part, op):
    pieces = [part[k : k + 8] for k in range(0, part.shape[0], 8)]
    while len(pieces) > 1:
        pieces = [op(*pieces[k : k + 2]) if k + 1 < len(pieces) else pieces[k] for k in range(0, len(pieces), 2)]
    return pieces[0]


def tile_kernel(plan, own_ref, *refs):
    n_new = len(plan["row_places"]) + len(plan["col_places"])
    tables, refs = refs[: plan["n_tables"]], refs[plan["n_tables"] :]
    arrived, refs = refs[:n_new], refs[n_new:]
    if plan["aliased"] or not plan["new"]:
        held, refs = refs[:3], refs[3:]
    if plan["new"]:
        loss_ref, held, refs = refs[0], refs[1:4], refs[4:]
    rows, cols, coeff = held
    row_out, refs = refs[: len(plan["row_outs"])], refs[len(plan["row_outs"]) :]
    col_out, (fresh, sem) = refs[: len(plan["col_outs"])], refs[len(plan["col_outs"]) :]
    width = rows.shape[1]
    inv_root = 1.0 / math.sqrt(width)
    size = tables[0].shape[0] // 2 if tables else 0

    targets = [rows.at[pl.ds(p, r.shape[0])] for p, r in zip(plan["row_places"], arrived)]
    targets += [cols.at[pl.ds(p, r.shape[0])] for p, r in zip(plan["col_places"], arrived[len(targets) :])]
    loads = [pltpu.make_async_copy(s, t, sem.at[k]) for k, (s, t) in enumerate(zip(arrived, targets))]
    for copy in loads:
        copy.start()
    for copy in loads:
        copy.wait()

    if plan["new"]:
        own = own_ref[0]
        loss = jnp.zeros((8, 128), jnp.float32)
        at, kept = 0, []
        for r0, r1, c0, c1 in plan["new"]:
            buffer = fresh.at[pl.ds(0, r1 - r0), pl.ds(at, c1 - c0)]
            at += c1 - c0
            kept.append((buffer, coeff.at[pl.ds(r0, r1 - r0), pl.ds(c0, c1 - c0)]))
            for cp, cl, j, c_off in plan["col_chunks"]:
                if cp < c0 or cp >= c1:
                    continue
                dots = (
                    lax.dot_general(
                        rows[r0:r1, :], cols[cp : cp + cl, :], (((1,), (1,)), ((), ())),
                        preferred_element_type=jnp.float32,
                    )
                    * inv_root
                )
                target = own ^ plan["col_xors"][j]
                for rp, rl, i, r_off in plan["row_chunks"]:
                    if rp < r0 or rp >= r1:
                        continue
                    scores = dots[rp - r0 : rp - r0 + rl]
                    pos, neg = tables[i][target], tables[i][size + target]
                    decay = jnp.exp(-jnp.abs(scores))
                    whole = 1.0 + decay
                    large = 1.0 / whole
                    up = scores >= 0.0
                    above = jnp.maximum(scores, 0.0)
                    if plan["row_xors"][i] == plan["col_xors"][j]:
                        later = lax.broadcasted_iota(jnp.int32, scores.shape, 1) + c_off > (
                            lax.broadcasted_iota(jnp.int32, scores.shape, 0) + r_off
                        )
                        pos = jnp.where(later, pos, 0.0)
                        soft = jnp.log(whole)
                        part = fold(pos * (above - scores + soft) + neg * (above + soft), jnp.add)
                    else:
                        over, total = fold(above, jnp.add), fold(scores, jnp.add)
                        part = neg * over + pos * (over - total)
                        part = part + (pos + neg) * jnp.log(fold(whole, jnp.multiply))
                    gain, drop = neg * inv_root, pos * inv_root
                    values = (jnp.where(up, gain, -drop) + jnp.where(up, -drop, gain) * decay) * large
                    for k in range(0, part.shape[1], 128):
                        loss = loss + part[:, k : k + 128]
                    buffer[rp - r0 : rp - r0 + rl, cp - c0 : cp - c0 + cl] = values.astype(jnp.bfloat16)
        loss_ref[...] = loss
        copies = [pltpu.make_async_copy(s, t, sem.at[n_new + k]) for k, (s, t) in enumerate(kept)]
        for copy in copies:
            copy.start()
        for copy in copies:
            copy.wait()

    def finish(outs, pieces, compute):
        if not outs:
            return
        low, high = min(p[0] for out in pieces for p in out), max(p[1] for out in pieces for p in out)
        for base in range(low, high, plan["step"]):
            top = min(high, base + plan["step"])
            value = compute(base, top)
            for out, parts in zip(outs, pieces):
                at = 0
                for p0, p1 in parts:
                    a, b = max(p0, base), min(p1, top)
                    if a < b:
                        out[at + a - p0 : at + b - p0, :] = value[a - base : b - base].astype(out.dtype)
                    at += p1 - p0

    finish(row_out, plan["row_outs"], lambda a, b: jnp.dot(
        coeff[a:b, :], cols[...], preferred_element_type=jnp.float32))
    finish(col_out, plan["col_outs"], lambda a, b: lax.dot_general(
        coeff[:, a:b], rows[...], (((0,), (0,)), ((), ())), preferred_element_type=jnp.float32))


def phase(own, tables, rows, cols, held, row_chunks, col_chunks, row_xors, col_xors, new=(), row_outs=(),
          col_outs=(), dtypes=None):
    n_row, n_col = (sum(c[1] for c in chunks) for chunks in (row_chunks, col_chunks))
    tables = tables if new else []
    width = next(iter(rows.values())).shape[1] if rows else held[0].shape[1]
    plan = dict(
        row_chunks=row_chunks, col_chunks=col_chunks, row_xors=row_xors, col_xors=col_xors, n_tables=len(tables),
        row_places=list(rows), col_places=list(cols), aliased=held is not None, new=new, row_outs=row_outs,
        col_outs=col_outs, step=512,
    )
    smem, anywhere, vmem = (pl.BlockSpec(memory_space=m) for m in (pltpu.SMEM, pl.ANY, pltpu.VMEM))
    args = [own, *tables, *rows.values(), *cols.values()]
    in_specs = [smem] * (1 + len(tables)) + [anywhere] * (len(rows) + len(cols))
    out_shape, aliases = [], {}
    if new:
        out_shape.append(pltpu.VMEM((8, 128), jnp.float32))
        if held is not None:
            aliases = {len(args) + k: 1 + k for k in range(3)}
        out_shape += [
            pltpu.VMEM(shape, jnp.bfloat16) for shape in ((n_row, width), (n_col, width), (n_row, n_col))
        ]
    if held is not None:
        args += [pltpu.with_memory_space_constraint(x, pltpu.VMEM) for x in held]
        in_specs += [vmem] * 3
    outs = (*row_outs, *col_outs)
    lengths = [sum(b - a for a, b in out) for out in outs]
    dtypes = dtypes or [jnp.bfloat16] * len(lengths)
    out_shape += [pltpu.VMEM((n, width), dtype) for n, dtype in zip(lengths, dtypes)]
    row_total, col_total = sum(lengths[: len(row_outs)]), sum(lengths[len(row_outs) :])
    area = sum((r1 - r0) * (c1 - c0) for r0, r1, c0, c1 in new)
    flops = 2 * width * (area + row_total * n_col + col_total * n_row)
    outs = list(
        pl.pallas_call(
            functools.partial(tile_kernel, plan),
            in_specs=in_specs,
            out_specs=[vmem] * len(out_shape),
            out_shape=out_shape,
            input_output_aliases=aliases,
            scratch_shapes=[
                pltpu.VMEM(
                    (max([16] + [r1 - r0 for r0, r1, _, _ in new]), max(128, sum(c1 - c0 for _, _, c0, c1 in new))),
                    jnp.bfloat16,
                ),
                pltpu.SemaphoreType.DMA((max(1, len(rows) + len(cols) + len(new)),)),
            ],
            cost_estimate=pl.CostEstimate(flops=flops, bytes_accessed=4 * width * width, transcendentals=2 * area),
            compiler_params=pltpu.CompilerParams(vmem_limit_bytes=20 << 20),
        )(*args)
    )
    loss = outs.pop(0) if new else None
    if new:
        held, outs = outs[:3], outs[3:]
    return loss, held, outs[: len(row_outs)], outs[len(row_outs) :]


def counts(pos_offset, neg_blocks, size):
    blocks = jnp.arange(size, dtype=jnp.int32)
    target = lax.axis_index(AXIS).astype(jnp.int32) + pos_offset.reshape(-1)
    pos = jnp.sum((target[:, None] == blocks).astype(jnp.float32), axis=0)
    neg = jnp.sum((neg_blocks.reshape(-1)[:, None] == blocks).astype(jnp.float32), axis=0)
    return jnp.concatenate([pos, neg])


def sum_kernel(groups, *refs):
    n_in = sum(len(group) for group in groups)
    ins, outs, totals, sem = list(refs[:n_in]), refs[n_in : n_in + len(groups)], refs[n_in + len(groups) : -1], refs[-1]
    n, stores = 64, []
    for starts, out, total in zip(groups, outs, totals):
        parts = [(start, ins.pop(0)) for start in starts]
        for r in range(0, out.shape[0], n):
            here = pl.ds(r, n)
            value = sum(
                part[r - start : r - start + n, :].astype(jnp.float32)
                for start, part in parts
                if start <= r < start + part.shape[0]
            )
            total[here] = value.reshape(n, *total.shape[1:])
            stores.append(pltpu.make_async_copy(total.at[here], out.at[here], sem.at[len(stores)]))
            stores[-1].start()
    for copy in stores:
        copy.wait()


def add_kernel(*refs):
    *parts, out = refs
    out[...] = sum(part[...].astype(jnp.float32) for part in parts).astype(out.dtype)


def add(*parts):
    vmem = pl.BlockSpec(memory_space=pltpu.VMEM)
    return pl.pallas_call(
        add_kernel,
        in_specs=[vmem] * len(parts),
        out_specs=vmem,
        out_shape=pltpu.VMEM(parts[0].shape, jnp.bfloat16),
        cost_estimate=pl.CostEstimate(
            flops=parts[0].size * len(parts), bytes_accessed=4 * parts[0].size, transcendentals=0
        ),
        compiler_params=pltpu.CompilerParams(vmem_limit_bytes=4 << 20),
    )(*[pltpu.with_memory_space_constraint(part, pltpu.VMEM) for part in parts])


def finish_sums(groups, length):
    width, lanes = groups[0][0][1].shape[1], 128
    anywhere, vmem = pl.BlockSpec(memory_space=pl.ANY), pl.BlockSpec(memory_space=pltpu.VMEM)
    flat = [part for group in groups for _, part in group]
    shape = (length, width // lanes, lanes)
    outs = pl.pallas_call(
        functools.partial(sum_kernel, [[start for start, _ in group] for group in groups]),
        in_specs=[vmem] * len(flat),
        out_specs=[anywhere] * len(groups),
        out_shape=[jax.ShapeDtypeStruct(shape, jnp.float32)] * len(groups),
        scratch_shapes=[pltpu.VMEM(shape, jnp.float32)] * len(groups)
        + [pltpu.SemaphoreType.DMA((len(groups) * (length // 64),))],
        cost_estimate=pl.CostEstimate(flops=6 * length * width, bytes_accessed=20 * length * width, transcendentals=0),
        compiler_params=pltpu.CompilerParams(vmem_limit_bytes=16 << 20),
    )(*[pltpu.with_memory_space_constraint(x, pltpu.VMEM) for x in flat])
    return [out.reshape(length, 1, width) for out in outs]


def step(states, goals, pos_offset, neg_blocks):
    size = lax.axis_size(AXIS)
    length, width = states.shape[0], states.shape[2]
    half = length // 2
    high = size // 2
    inner = []
    bit = size // 4
    while bit > 1:
        inner.append(bit)
        bit //= 2
    across = high ^ (high >> 1)
    row_xors, col_xors = [0, 1, across, across ^ 1], subsets(inner)
    n_row, n_col = len(row_xors) * length, len(col_xors) * length
    last = n_col - length
    state, goal = states.reshape(length, width), goals.reshape(length, width)
    own = lax.axis_index(AXIS).astype(jnp.int32).reshape(1)

    cols = {0: goal}
    for bit in inner:
        shift = len(cols) * length
        cols = {**cols, **{p + shift: swap(c, bit, size) for p, c in cols.items()}}
    sib = swap(state, 1, size)


    def outer(i):
        return (i & across) in (0, across)

    pair_in = swap(state, across, size, lambda i: not outer(i))
    pair = pair_in + swap(state, across, size, outer)
    far = swap(pair, 1, size)
    table = counts(pos_offset, neg_blocks, size)
    tables = [table] + [swap(table, x, size) for x in row_xors[1:]]

    near, third = 2 * length, 3 * length
    row_chunks = tuple((k * length, length, k, 0) for k in range(len(row_xors)))
    col_chunks = tuple((k * length, length, k, 0) for k in range(len(col_xors)))
    fixed = dict(row_chunks=row_chunks, col_chunks=col_chunks, row_xors=row_xors, col_xors=col_xors)
    early = {p: c for p, c in cols.items() if 0 < p < last}
    loss_a, held, _, _ = phase(
        own, tables[:2], {0: state, length: sib}, {0: goal}, None, new=[(0, near, 0, length)], **fixed
    )
    loss_b, held, _, _ = phase(own, tables[:2], {}, early, held, new=[(0, near, length, last)], **fixed)
    loss_e, held, _, _ = phase(own, tables[:2], {}, {last: cols[last]}, held, new=[(0, near, last, n_col)], **fixed)
    first = n_col // 2
    soon_cols = [[(first, first + half)], [(first + half, first + length)]]
    loss_c, held, _, soon = phase(
        own, tables, {near: pair, third: far}, {}, held, new=[(near, n_row, 0, last)], col_outs=soon_cols, **fixed
    )
    loss_d, held, (far_part, pair_part), _ = phase(
        own, tables, {}, {}, held, new=[(near, n_row, last, n_col)],
        row_outs=[[(third, n_row)], [(near, third)]], **fixed,
    )
    loss = loss_a + loss_b + loss_c + loss_d + loss_e

    back_far = swap(far_part, 1, size)
    loss = loss + swap(loss, across, size)
    back_pair = swap(add(pair_part, back_far), across, size)
    sent_cols = [[(p, p + half)] for p in range(first + length, n_col, half)]
    _, _, _, sent = phase(own, [], {}, {}, held, col_outs=sent_cols, **fixed)
    parts = {out[0][0]: value for out, value in zip([*soon_cols, *sent_cols], [*soon, *sent])}
    kept_cols = [[(0, length)]] + [[(p, p + half)] for p in range(length, n_col // 2, half)]
    _, _, (own_part, sib_part), kept = phase(
        own, [], {}, {}, held, row_outs=[[(0, length)], [(length, near)]], col_outs=kept_cols,
        dtypes=[jnp.float32, jnp.bfloat16] + [jnp.float32] * len(kept_cols), **fixed,
    )
    parts.update({out[0][0]: value for out, value in zip(kept_cols, kept)})
    back_sib = swap(sib_part, 1, size)
    for k, bit in reversed(list(enumerate(inner))):
        loss = loss + swap(loss, bit, size)
    loss = loss + swap(loss, 1, size)
    got = {}
    for k in reversed(range(len(inner))):
        lower = length << k
        for p in sorted(p - lower for p in parts if p >= lower)[::-1]:
            mine = parts.pop(p + lower)
            if p + lower in got:
                mine = add(mine, *got.pop(p + lower))
            got.setdefault(p, []).append(swap(mine, inner[k], size))
    goal_parts = [(0, parts[0])] + [(p, part) for p, received in got.items() for part in received]
    grad_states, grad_goals = finish_sums([[(0, own_part), (0, back_sib), (0, back_pair)], goal_parts], length)
    loss_mean = jnp.sum(loss).reshape(1) / (size * length)
    return (loss_mean, grad_states, grad_goals)


def solution(mesh):
    spec = P("tm", "groups", None)
    return jax.shard_map(
        step,
        mesh=mesh,
        in_specs=(spec,) * 4,
        out_specs=(P("groups"), spec, spec),
        check_vma=False,
    )
```

time: 220 us -> 99.9 us (0.45)
  waiting for transfers between devices: 138 us -> 50.7 us
  blocking collectives: 32.1 us -> 0 us
  matrix products: 25.9 us -> 0 us
  starting transfers between devices: 0.08 us -> 22 us
  Pallas kernels: 0 us -> 19.8 us
  between operations: 15.9 us -> 2.6 us
  local copies, waits for them, and re-layouts: 6.8 us -> 2.08 us
    all_gather x1 -> x0, waiting for transfers between devices: 77.6 us -> none  [per_device(): goal_piece = lax.all_gather(goals, 'tm', axis=0, tiled=True)]
    reduce_scatter x1 -> x0, waiting for transfers between devices: 59.2 us -> none  [per_device(): lax.psum_scatter(jnp.einsum('tqk,qte->kte', coeff_all, states, preferred_...]
    ppermute x0 -> x23, waiting for transfers between devices: none -> 50.7 us  [swap(): lax.ppermute(value, AXIS, [(i, i ^ offset) for i in range(size) if only(i)])]
    psum x1 -> x0, blocking collectives: 32.1 us -> none  [per_device(): loss_all = lax.psum(loss_sum, 'tm')]
    dot_general x3 -> x0, matrix products: 25.9 us -> none  [the longest x1 11.5 us: score_terms(): jnp.einsum('qte,kte->tqk', anchor_rows, goal_rows, preferred_element_type...]
    ppermute x0 -> x23, starting transfers between devices: none -> 22 us  [swap(): lax.ppermute(value, AXIS, [(i, i ^ offset) for i in range(size) if only(i)])]
    pallas_call x0 -> x11, Pallas kernels: none -> 19.8 us  [the longest x7 15.5 us: phase(): pl.pallas_call(functools.partial(tile_kernel, plan), in_specs=in_specs, o...]
    unnamed x6 -> x4, local copies, waits for them, and re-layouts: 6.8 us -> 2.08 us
  transfers between devices with their start and end apart: 2 -> 23, of which waited for: 2 -> 12; matrix products, arithmetic and copies ran while one was open for 5% -> 2% of each run, Pallas kernels for 0% -> 10%
where the time goes in v2:
time: 99.9 us; the launch traced here: 99.5 us
  waiting for transfers between devices  50.7 us (51%)
  starting transfers between devices  22 us (22%)
  Pallas kernels  19.8 us (20%)
  between operations  2.6 us (3%)
  other arithmetic  2.37 us (2%)
  local copies, waits for them, and re-layouts  2.08 us (2%)
    ppermute x23, waiting for transfers between devices, swap(): lax.ppermute(value, AXIS, [(i, i ^ offset) for i in range(size) if only(i)])  50.7 us
    ppermute x23, starting transfers between devices, swap(): lax.ppermute(value, AXIS, [(i, i ^ offset) for i in range(size) if only(i)])  22 us
    pallas_call x7, Pallas kernels, phase(): pl.pallas_call(functools.partial(tile_kernel, plan), in_specs=in_specs, o...  15.5 us
    pallas_call x1, Pallas kernels, finish_sums(): pl.pallas_call(functools.partial(sum_kernel, [[start for start, _ in grou...  2.71 us
    unnamed x4, local copies, waits for them, and re-layouts  2.08 us
  transfers between devices with their start and end apart: 23, of which 12 were waited for; matrix products, arithmetic and copies ran while one was open for 2% of the time, Pallas kernels for 10%

profile of v2, /device:TPU:0, one launch (start us, length us, event | category | flops | bytes accessed | tf_op | source)
XLA Modules:
  0.0 99.5 jit_solution(2122095182016525235)
XLA Ops:
  0.6 0.7 collective-permute-start.6
  1.3 7.0 %collective-permute-start.7 = (bf16[256,1024]{1,0:T(8,128)(2,1)}, bf16[256,1024]{1,0:T(8,128)(2,1)S(1)}, u32[]{:S(2)}, u32[]{:S(2)}) collective-permute-start(bf16[256,1024]{1,0:T(8,128)(2,1)} %bitcast.10), channel_id=1, source_target_pairs={{0,12},{1,13},{2,14},{3,15},{12,0},{13,1},{14,2},{15,3},{16,28},{1... | collective-permute-start | bytes 1572872 | tf_op jit(solution)/shard_map/ppermute | solution.py:16
  8.3 0.1 collective-permute-start.2
  8.4 1.6 %collective-permute-start.3 = (bf16[256,1024]{1,0:T(8,128)(2,1)}, bf16[256,1024]{1,0:T(8,128)(2,1)S(1)}, u32[]{:S(2)}, u32[]{:S(2)}) collective-permute-start(bf16[256,1024]{1,0:T(8,128)(2,1)} %bitcast.14), channel_id=1, source_target_pairs={{0,2},{1,3},{2,0},{3,1},{4,6},{5,7},{6,4},{7,5},{8,10},{9,11},{10,... | collective-permute-start | bytes 1572872 | tf_op jit(solution)/shard_map/ppermute | solution.py:16
  10.0 0.7 convert_reduce_fusion
  10.7 10.6 %collective-permute-done.7 = bf16[256,1024]{1,0:T(8,128)(2,1)S(1)} collective-permute-done((bf16[256,1024]{1,0:T(8,128)(2,1)}, bf16[256,1024]{1,0:T(8,128)(2,1)S(1)}, u32[]{:S(2)}, u32[]{:S(2)}) %collective-permute-start.7) | collective-permute-done | bytes 524320 | tf_op jit(solution)/shard_map/ppermute | solution.py:16
  21.4 0.2 add.44.refs_4_
  21.6 0.1 collective-permute-start.8
  21.7 10.1 %collective-permute-done.2.refs_2_ = bf16[256,1024]{1,0:T(8,128)(2,1)S(1)} collective-permute-done((bf16[256,1024]{1,0:T(8,128)(2,1)}, bf16[256,1024]{1,0:T(8,128)(2,1)S(1)}, u32[]{:S(2)}, u32[]{:S(2)}) %collective-permute-start.2) | collective-permute-done | bytes 524320 | tf_op jit(solution)/shard_map/ppermute | solution.py:16
  31.8 1.5 %collective-permute-start.9 = (bf16[256,1024]{1,0:T(8,128)(2,1)S(1)}, bf16[256,1024]{1,0:T(8,128)(2,1)S(1)}, u32[]{:S(2)}, u32[]{:S(2)}) collective-permute-start(bf16[256,1024]{1,0:T(8,128)(2,1)S(1)} %collective-permute-done.2.refs_2_), channel_id=1, source_target_pairs={{0,2},{1,3},{2,0},{3,1},{4,6},{5,7},{6,4},{7,5},{8,10},{9,11},{10,... | collective-permute-start | bytes 1572872 | tf_op jit(solution)/shard_map/ppermute | solution.py:16
  33.3 0.7 add_bitcast_fusion
  34.0 0.1 convert_reduce_fusion.1
  34.0 0.1 pad_maximum_fusion.refs_0_
  34.1 1.2 %collective-permute-done.refs_1_ = f32[32]{0:T(128)S(1)} collective-permute-done((f32[32]{0:T(128)S(1)}, f32[32]{0:T(128)S(1)}, u32[]{:S(2)}, u32[]{:S(2)}) %collective-permute-start) | collective-permute-done | bytes 160 | tf_op jit(solution)/shard_map/ppermute | solution.py:16
  35.3 1.7 %collective-permute-start.4 = (f32[32]{0:T(128)S(1)}, f32[32]{0:T(128)S(1)}, u32[]{:S(2)}, u32[]{:S(2)}) collective-permute-start(f32[32]{0:T(128)S(1)} %pad_maximum_fusion.refs_0_), channel_id=1, source_target_pairs={{0,12},{1,13},{2,14},{3,15},{4,8},{5,9},{6,10},{7,11},{8,4},{9,5},... | collective-permute-start | bytes 392 | tf_op jit(solution)/shard_map/ppermute | solution.py:16
  37.0 1.6 %collective-permute-start.5 = (f32[32]{0:T(128)S(1)}, f32[32]{0:T(128)S(1)}, u32[]{:S(2)}, u32[]{:S(2)}) collective-permute-start(f32[32]{0:T(128)S(1)} %pad_maximum_fusion.refs_0_), channel_id=1, source_target_pairs={{0,13},{1,12},{2,15},{3,14},{4,9},{5,8},{6,11},{7,10},{8,5},{9,4},... | collective-permute-start | bytes 392 | tf_op jit(solution)/shard_map/ppermute | solution.py:16
  38.6 1.0 %copy-done = bf16[256,1,1024]{2,0,1:T(8,128)(2,1)S(1)} copy-done((bf16[256,1,1024]{2,0,1:T(8,128)(2,1)S(1)}, bf16[256,1,1024]{2,0,1:T(8,128)(2,1)}, u32[]{:S(2)}) %copy-start) | copy-done | bytes 524312
  39.7 1.0 %copy-done.1 = bf16[256,1,1024]{2,0,1:T(8,128)(2,1)S(1)} copy-done((bf16[256,1,1024]{2,0,1:T(8,128)(2,1)S(1)}, bf16[256,1,1024]{2,0,1:T(8,128)(2,1)}, u32[]{:S(2)}) %copy-start.1) | copy-done | bytes 524312
  40.7 1.5 %shard_map.67 = (f32[8,128]{1,0:T(8,128)S(1)}, bf16[1024,1024]{1,0:T(8,128)(2,1)S(1)}, bf16[1024,1024]{1,0:T(8,128)(2,1)S(1)}, bf16[1024,1024]{1,0:T(8,128)(2,1)S(1)}) custom-call(s32[1]{0:T(128)} %bitcast.own_ref, f32[32]{0:T(128)S(1)} %pad_maximum_fusion.refs_0_, f32[32]{0:T(128)S(1)} %collective-permute-done.refs_1_, bf16[256,1024]{1,0:T(8,128)(2,1)S(1)} %bitcast.12, ...), custom_call_target="tpu_custom_call" | custom-call | flops 268435456 | bytes 4194304 | tf_op jit(solution)/shard_map/pallas_call | solution.py:161
  42.2 2.0 %shard_map.68 = (f32[8,128]{1,0:T(8,128)S(1)}, bf16[1024,1024]{1,0:T(8,128)(2,1)S(1)}, bf16[1024,1024]{1,0:T(8,128)(2,1)S(1)}, bf16[1024,1024]{1,0:T(8,128)(2,1)S(1)}) custom-call(s32[1]{0:T(128)} %bitcast.own_ref, f32[32]{0:T(128)S(1)} %pad_maximum_fusion.refs_0_, ...), custom_call_target="tpu_custom_call", output_to_operand_aliasing={{1}: (5, {}), {2}: (6, {}), {3}: (7, {})} | custom-call | flops 536870912 | bytes 4194304 | tf_op jit(solution)/shard_map/pallas_call | solution.py:161
  44.2 1.4 %collective-permute-done.9.refs_2_ = bf16[256,1024]{1,0:T(8,128)(2,1)S(1)} collective-permute-done((bf16[256,1024]{1,0:T(8,128)(2,1)S(1)}, bf16[256,1024]{1,0:T(8,128)(2,1)S(1)}, u32[]{:S(2)}, u32[]{:S(2)}) %collective-permute-start.9) | collective-permute-done | bytes 524320 | tf_op jit(solution)/shard_map/ppermute | solution.py:16
  45.6 1.3 %shard_map.69 = (f32[8,128]{1,0:T(8,128)S(1)}, bf16[1024,1024]{1,0:T(8,128)(2,1)S(1)}, bf16[1024,1024]{1,0:T(8,128)(2,1)S(1)}, bf16[1024,1024]{1,0:T(8,128)(2,1)S(1)}) custom-call(s32[1]{0:T(128)} %bitcast.own_ref, f32[32]{0:T(128)S(1)} %pad_maximum_fusion.refs_0_, ...), custom_call_target="tpu_custom_call", output_to_operand_aliasing={{1}: (4, {}), {2}: (5, {}), {3}: (6, {})} | custom-call | flops 268435456 | bytes 4194304 | tf_op jit(solution)/shard_map/pallas_call | solution.py:161
  47.0 4.5 %shard_map.70 = (f32[8,128]{1,0:T(8,128)S(1)}, bf16[1024,1024]{1,0:T(8,128)(2,1)S(1)}, bf16[1024,1024]{1,0:T(8,128)(2,1)S(1)}, bf16[1024,1024]{1,0:T(8,128)(2,1)...) custom-call(s32[1]{0:T(128)} %bitcast.own_ref, ...), custom_call_target="tpu_custom_call", output_to_operand_aliasing={{1}: (7, {}), {2}: (8, {}), {3}: (9, {})} | custom-call | flops 1342177280 | bytes 4194304 | tf_op jit(solution)/shard_map/pallas_call | solution.py:161
  51.5 3.1 %shard_map.71 = (f32[8,128]{1,0:T(8,128)S(1)}, bf16[1024,1024]{1,0:T(8,128)(2,1)S(1)}, bf16[1024,1024]{1,0:T(8,128)(2,1)S(1)}, bf16[1024,1024]{1,0:T(8,128)(2,1)...) custom-call(s32[1]{0:T(128)} %bitcast.own_ref, ...), custom_call_target="tpu_custom_call", output_to_operand_aliasing={{1}: (5, {}), {2}: (6, {}), {3}: (7, {})} | custom-call | flops 1342177280 | bytes 4194304 | tf_op jit(solution)/shard_map/pallas_call | solution.py:161
  54.5 0.1 collective-permute-start.15
  54.6 0.9 collective-permute-start.10
  55.5 4.6 %collective-permute-done.10 = f32[8,128]{1,0:T(8,128)S(1)} collective-permute-done((f32[8,128]{1,0:T(8,128)S(1)}, f32[8,128]{1,0:T(8,128)S(1)}, u32[]{:S(2)}, u32[]{:S(2)}) %collective-permute-start.10) | collective-permute-done | bytes 4128 | tf_op jit(solution)/shard_map/ppermute | solution.py:16
  60.1 1.5 %collective-permute-start.11 = (f32[8,128]{1,0:T(8,128)S(1)}, f32[8,128]{1,0:T(8,128)S(1)}, u32[]{:S(2)}, u32[]{:S(2)}) collective-permute-start(f32[8,128]{1,0:T(8,128)S(1)} %add.48), channel_id=1, source_target_pairs={{0,2},{1,3},{2,0},{3,1},{4,6},{5,7},{6,4},{7,5},{8,10},{9,11},{10,... | collective-permute-start | bytes 12296 | tf_op jit(solution)/shard_map/ppermute | solution.py:16
  61.6 0.8 shard_map.74
  62.4 0.6 collective-permute-start.18
  63.0 0.7 collective-permute-done.11
  63.7 2.4 %shard_map.72 = (f32[256,1024]{1,0:T(8,128)S(1)}, bf16[256,1024]{1,0:T(8,128)(2,1)}, f32[256,1024]{1,0:T(8,128)S(1)}, f32[128,1024]{1,0:T(8,128)S(1)}, f32[128,1024]{1,0:T(8,128)S(1)}) custom-call(s32[1]{0:T(128)} %bitcast.own_ref, bf16[1024,1024]{1,0:T(8,128)(2,1)S(1)} %get-tuple-element.53.refs_0_, bf16[1024,1024]{1,0:T(8,128)(2,1)S(1)} %get-tuple-element.54.refs_1_, ...), custom_call_target="tpu_custom_call" | custom-call | flops 2147483648 | bytes 4194304 | tf_op jit(solution)/shard_map/pallas_call | solution.py:161
  66.1 1.6 %collective-permute-start.21 = (bf16[128,1024]{1,0:T(8,128)(2,1)S(1)}, bf16[128,1024]{1,0:T(8,128)(2,1)S(1)}, u32[]{:S(2)}, u32[]{:S(2)}) collective-permute-start(bf16[128,1024]{1,0:T(8,128)(2,1)S(1)} %get-tuple-element.66), channel_id=1, source_target_pairs={{0,2},{1,3},{2,0},{3,1},{4,6},{5,7},{6,4},{7,5},{8,10},{9,11},{10,... | collective-permute-start | bytes 786440 | tf_op jit(solution)/shard_map/ppermute | solution.py:16
  67.7 0.5 collective-permute-start.17
  68.2 0.1 shard_map.73
  68.3 0.9 collective-permute-start.16
  69.3 2.4 %collective-permute-done.18.refs_1_ = bf16[128,1024]{1,0:T(8,128)(2,1)S(1)} collective-permute-done((bf16[128,1024]{1,0:T(8,128)(2,1)S(1)}, bf16[128,1024]{1,0:T(8,128)(2,1)S(1)}, u32[]{:S(2)}, u32[]{:S(2)}) %collective-permute-start.18) | collective-permute-done | bytes 262176 | tf_op jit(solution)/shard_map/ppermute | solution.py:16
  71.6 0.7 shard_map.75
  72.4 4.9 %collective-permute-done.21.refs_1_ = bf16[128,1024]{1,0:T(8,128)(2,1)S(1)} collective-permute-done((bf16[128,1024]{1,0:T(8,128)(2,1)S(1)}, bf16[128,1024]{1,0:T(8,128)(2,1)S(1)}, u32[]{:S(2)}, u32[]{:S(2)}) %collective-permute-start.21) | collective-permute-done | bytes 262176 | tf_op jit(solution)/shard_map/ppermute | solution.py:16
  77.3 0.4 collective-permute-start.20
  77.6 0.8 shard_map.76
  78.4 1.3 %collective-permute-start.19 = (bf16[128,1024]{1,0:T(8,128)(2,1)}, bf16[128,1024]{1,0:T(8,128)(2,1)}, u32[]{:S(2)}, u32[]{:S(2)}) collective-permute-start(bf16[128,1024]{1,0:T(8,128)(2,1)} %shard_map.75), channel_id=1, source_target_pairs={{0,4},{1,5},{2,6},{3,7},{4,0},{5,1},{6,2},{7,3},{8,12},{9,13},{10,... | collective-permute-start | bytes 786440 | tf_op jit(solution)/shard_map/ppermute | solution.py:16
  79.7 3.2 %collective-permute-done.17.refs_4_ = bf16[128,1024]{1,0:T(8,128)(2,1)S(1)} collective-permute-done((bf16[128,1024]{1,0:T(8,128)(2,1)S(1)}, bf16[128,1024]{1,0:T(8,128)(2,1)S(1)}, u32[]{:S(2)}, u32[]{:S(2)}) %collective-permute-start.17) | collective-permute-done | bytes 262176 | tf_op jit(solution)/shard_map/ppermute | solution.py:16
  82.9 0.6 add_reduce_fusion
  84.1 2.5 %collective-permute-done.20.refs_6_ = bf16[128,1024]{1,0:T(8,128)(2,1)} collective-permute-done((bf16[128,1024]{1,0:T(8,128)(2,1)}, bf16[128,1024]{1,0:T(8,128)(2,1)}, u32[]{:S(2)}, u32[]{:S(2)}) %collective-permute-start.20) | collective-permute-done | bytes 262176 | tf_op jit(solution)/shard_map/ppermute | solution.py:16
  86.6 3.5 %collective-permute-done.19.refs_5_ = bf16[128,1024]{1,0:T(8,128)(2,1)} collective-permute-done((bf16[128,1024]{1,0:T(8,128)(2,1)}, bf16[128,1024]{1,0:T(8,128)(2,1)}, u32[]{:S(2)}, u32[]{:S(2)}) %collective-permute-start.19) | collective-permute-done | bytes 262176 | tf_op jit(solution)/shard_map/ppermute | solution.py:16
  90.2 5.5 %collective-permute-done.22.refs_7_ = bf16[128,1024]{1,0:T(8,128)(2,1)} collective-permute-done((bf16[128,1024]{1,0:T(8,128)(2,1)}, bf16[128,1024]{1,0:T(8,128)(2,1)}, u32[]{:S(2)}, u32[]{:S(2)}) %collective-permute-start.22) | collective-permute-done | bytes 262176 | tf_op jit(solution)/shard_map/ppermute | solution.py:16
  95.7 2.7 %shard_map.77 = (f32[256,8,128]{2,1,0:T(8,128)}, f32[256,8,128]{2,1,0:T(8,128)}) custom-call(f32[256,1024]{1,0:T(8,128)S(1)} %get-tuple-element.56.refs_0_, bf16[256,1024]{1,0:T(8,128)(2,1)S(1)} %collective-permute-done.14.refs_1_, bf16[256,1024]{1,0:T(8,128)(2,1)} %collective-permute-done.16.refs_2_, f32[256,1024]{1,0:T(8,128)S(1)} %get-tuple-element.60.refs_3_, ...), custom_call_target="tpu_custom_call" | custom-call | flops 1572864 | bytes 5242880 | tf_op jit(solution)/shard_map/pallas_call | solution.py:236
  (23 shorter events, 0.1 us)
Async XLA Ops:
  0.6 10.1 %collective-permute-start.6 = (bf16[256,1024]{1,0:T(8,128)(2,1)}, bf16[256,1024]{1,0:T(8,128)(2,1)S(1)}, u32[]{:S(2)}, u32[]{:S(2)}) collective-permute-start(bf16[256,1024]{1,0:T(8,128)(2,1)} %bitcast.9), channel_id=1, source_target_pairs={{4,8},{5,9},{6,10},{7,11},{8,4},{9,5},{10,6},{11,7},{20,24},{21,25... | collective-permute-start | bytes 1572872 | tf_op jit(solution)/shard_map/ppermute | solution.py:16
  1.3 20.1 %collective-permute-start.7 = (bf16[256,1024]{1,0:T(8,128)(2,1)}, bf16[256,1024]{1,0:T(8,128)(2,1)S(1)}, u32[]{:S(2)}, u32[]{:S(2)}) collective-permute-start(bf16[256,1024]{1,0:T(8,128)(2,1)} %bitcast.10), channel_id=1, source_target_pairs={{0,12},{1,13},{2,14},{3,15},{12,0},{13,1},{14,2},{15,3},{16,28},{1... | collective-permute-start | bytes 1572872 | tf_op jit(solution)/shard_map/ppermute | solution.py:16
  8.3 23.5 %collective-permute-start.2 = (bf16[256,1024]{1,0:T(8,128)(2,1)}, bf16[256,1024]{1,0:T(8,128)(2,1)S(1)}, u32[]{:S(2)}, u32[]{:S(2)}) collective-permute-start(bf16[256,1024]{1,0:T(8,128)(2,1)} %bitcast.13), channel_id=1, source_target_pairs={{0,4},{1,5},{2,6},{3,7},{4,0},{5,1},{6,2},{7,3},{8,12},{9,13},{10,... | collective-permute-start | bytes 1572872 | tf_op jit(solution)/shard_map/ppermute | solution.py:16
  8.4 33.8 %collective-permute-start.3 = (bf16[256,1024]{1,0:T(8,128)(2,1)}, bf16[256,1024]{1,0:T(8,128)(2,1)S(1)}, u32[]{:S(2)}, u32[]{:S(2)}) collective-permute-start(bf16[256,1024]{1,0:T(8,128)(2,1)} %bitcast.14), channel_id=1, source_target_pairs={{0,2},{1,3},{2,0},{3,1},{4,6},{5,7},{6,4},{7,5},{8,10},{9,11},{10,... | collective-permute-start | bytes 1572872 | tf_op jit(solution)/shard_map/ppermute | solution.py:16
  10.0 27.0 %collective-permute-start.1 = (bf16[256,1024]{1,0:T(8,128)(2,1)}, bf16[256,1024]{1,0:T(8,128)(2,1)S(1)}, u32[]{:S(2)}, u32[]{:S(2)}) collective-permute-start(bf16[256,1024]{1,0:T(8,128)(2,1)} %bitcast.11), channel_id=1, source_target_pairs={{0,1},{1,0},{2,3},{3,2},{4,5},{5,4},{6,7},{7,6},{8,9},{9,8},{10,11... | collective-permute-start | bytes 1572872 | tf_op jit(solution)/shard_map/ppermute | solution.py:16
  21.6 25.4 %collective-permute-start.8 = (bf16[256,1024]{1,0:T(8,128)(2,1)S(1)}, bf16[256,1024]{1,0:T(8,128)(2,1)S(1)}, u32[]{:S(2)}, u32[]{:S(2)}) collective-permute-start(bf16[256,1024]{1,0:T(8,128)(2,1)S(1)} %add.44.refs_4_), channel_id=1, source_target_pairs={{0,1},{1,0},{2,3},{3,2},{4,5},{5,4},{6,7},{7,6},{8,9},{9,8},{10,11... | collective-permute-start | bytes 1572872 | tf_op jit(solution)/shard_map/ppermute | solution.py:16
  31.8 13.8 %collective-permute-start.9 = (bf16[256,1024]{1,0:T(8,128)(2,1)S(1)}, bf16[256,1024]{1,0:T(8,128)(2,1)S(1)}, u32[]{:S(2)}, u32[]{:S(2)}) collective-permute-start(bf16[256,1024]{1,0:T(8,128)(2,1)S(1)} %collective-permute-done.2.refs_2_), channel_id=1, source_target_pairs={{0,2},{1,3},{2,0},{3,1},{4,6},{5,7},{6,4},{7,5},{8,10},{9,11},{10,... | collective-permute-start | bytes 1572872 | tf_op jit(solution)/shard_map/ppermute | solution.py:16
  34.1 1.2 %collective-permute-start = (f32[32]{0:T(128)S(1)}, f32[32]{0:T(128)S(1)}, u32[]{:S(2)}, u32[]{:S(2)}) collective-permute-start(f32[32]{0:T(128)S(1)} %pad_maximum_fusion.refs_0_), channel_id=1, source_target_pairs={{0,1},{1,0},{2,3},{3,2},{4,5},{5,4},{6,7},{7,6},{8,9},{9,8},{10,11... | collective-permute-start | bytes 392 | tf_op jit(solution)/shard_map/ppermute | solution.py:16
  35.3 11.7 %collective-permute-start.4 = (f32[32]{0:T(128)S(1)}, f32[32]{0:T(128)S(1)}, u32[]{:S(2)}, u32[]{:S(2)}) collective-permute-start(f32[32]{0:T(128)S(1)} %pad_maximum_fusion.refs_0_), channel_id=1, source_target_pairs={{0,12},{1,13},{2,14},{3,15},{4,8},{5,9},{6,10},{7,11},{8,4},{9,5},... | collective-permute-start | bytes 392 | tf_op jit(solution)/shard_map/ppermute | solution.py:16
  37.0 9.9 %collective-permute-start.5 = (f32[32]{0:T(128)S(1)}, f32[32]{0:T(128)S(1)}, u32[]{:S(2)}, u32[]{:S(2)}) collective-permute-start(f32[32]{0:T(128)S(1)} %pad_maximum_fusion.refs_0_), channel_id=1, source_target_pairs={{0,13},{1,12},{2,15},{3,14},{4,9},{5,8},{6,11},{7,10},{8,5},{9,4},... | collective-permute-start | bytes 392 | tf_op jit(solution)/shard_map/ppermute | solution.py:16
  38.6 1.0 %copy-start = (bf16[256,1,1024]{2,0,1:T(8,128)(2,1)S(1)}, bf16[256,1,1024]{2,0,1:T(8,128)(2,1)}, u32[]{:S(2)}) copy-start(bf16[256,1,1024]{2,0,1:T(8,128)(2,1)} %param.4) | copy-start | bytes 1572868
  39.6 1.0 %copy-start.1 = (bf16[256,1,1024]{2,0,1:T(8,128)(2,1)S(1)}, bf16[256,1,1024]{2,0,1:T(8,128)(2,1)}, u32[]{:S(2)}) copy-start(bf16[256,1,1024]{2,0,1:T(8,128)(2,1)} %param.5) | copy-start | bytes 1572868
  54.5 13.2 %collective-permute-start.15 = (bf16[256,1024]{1,0:T(8,128)(2,1)S(1)}, bf16[256,1024]{1,0:T(8,128)(2,1)S(1)}, u32[]{:S(2)}, u32[]{:S(2)}) collective-permute-start(bf16[256,1024]{1,0:T(8,128)(2,1)S(1)} %get-tuple-element.59), channel_id=1, source_target_pairs={{0,1},{1,0},{2,3},{3,2},{4,5},{5,4},{6,7},{7,6},{8,9},{9,8},{10,11... | collective-permute-start | bytes 1572872 | tf_op jit(solution)/shard_map/ppermute | solution.py:16
  54.6 5.5 %collective-permute-start.10 = (f32[8,128]{1,0:T(8,128)S(1)}, f32[8,128]{1,0:T(8,128)S(1)}, u32[]{:S(2)}, u32[]{:S(2)}) collective-permute-start(f32[8,128]{1,0:T(8,128)S(1)} %add_add_fusion), channel_id=1, source_target_pairs={{0,12},{1,13},{2,14},{3,15},{4,8},{5,9},{6,10},{7,11},{8,4},{9,5},... | collective-permute-start | bytes 12296 | tf_op jit(solution)/shard_map/ppermute | solution.py:16
  60.1 3.6 %collective-permute-start.11 = (f32[8,128]{1,0:T(8,128)S(1)}, f32[8,128]{1,0:T(8,128)S(1)}, u32[]{:S(2)}, u32[]{:S(2)}) collective-permute-start(f32[8,128]{1,0:T(8,128)S(1)} %add.48), channel_id=1, source_target_pairs={{0,2},{1,3},{2,0},{3,1},{4,6},{5,7},{6,4},{7,5},{8,10},{9,11},{10,... | collective-permute-start | bytes 12296 | tf_op jit(solution)/shard_map/ppermute | solution.py:16
  62.4 9.2 %collective-permute-start.18 = (bf16[128,1024]{1,0:T(8,128)(2,1)S(1)}, bf16[128,1024]{1,0:T(8,128)(2,1)S(1)}, u32[]{:S(2)}, u32[]{:S(2)}) collective-permute-start(bf16[128,1024]{1,0:T(8,128)(2,1)S(1)} %get-tuple-element.63), channel_id=1, source_target_pairs={{0,2},{1,3},{2,0},{3,1},{4,6},{5,7},{6,4},{7,5},{8,10},{9,11},{10,... | collective-permute-start | bytes 786440 | tf_op jit(solution)/shard_map/ppermute | solution.py:16
  63.7 4.6 %collective-permute-start.12 = (f32[8,128]{1,0:T(8,128)S(1)}, f32[8,128]{1,0:T(8,128)S(1)}, u32[]{:S(2)}, u32[]{:S(2)}) collective-permute-start(f32[8,128]{1,0:T(8,128)S(1)} %add.49), channel_id=1, source_target_pairs={{0,4},{1,5},{2,6},{3,7},{4,0},{5,1},{6,2},{7,3},{8,12},{9,13},{10,... | collective-permute-start | bytes 12296 | tf_op jit(solution)/shard_map/ppermute | solution.py:16
  66.1 11.2 %collective-permute-start.21 = (bf16[128,1024]{1,0:T(8,128)(2,1)S(1)}, bf16[128,1024]{1,0:T(8,128)(2,1)S(1)}, u32[]{:S(2)}, u32[]{:S(2)}) collective-permute-start(bf16[128,1024]{1,0:T(8,128)(2,1)S(1)} %get-tuple-element.66), channel_id=1, source_target_pairs={{0,2},{1,3},{2,0},{3,1},{4,6},{5,7},{6,4},{7,5},{8,10},{9,11},{10,... | collective-permute-start | bytes 786440 | tf_op jit(solution)/shard_map/ppermute | solution.py:16
  67.7 18.9 %collective-permute-start.14 = (bf16[256,1024]{1,0:T(8,128)(2,1)}, bf16[256,1024]{1,0:T(8,128)(2,1)S(1)}, u32[]{:S(2)}, u32[]{:S(2)}) collective-permute-start(bf16[256,1024]{1,0:T(8,128)(2,1)} %get-tuple-element.57), channel_id=1, source_target_pairs={{0,1},{1,0},{2,3},{3,2},{4,5},{5,4},{6,7},{7,6},{8,9},{9,8},{10,11... | collective-permute-start | bytes 1572872 | tf_op jit(solution)/shard_map/ppermute | solution.py:16
  67.7 15.1 %collective-permute-start.17 = (bf16[128,1024]{1,0:T(8,128)(2,1)S(1)}, bf16[128,1024]{1,0:T(8,128)(2,1)S(1)}, u32[]{:S(2)}, u32[]{:S(2)}) collective-permute-start(bf16[128,1024]{1,0:T(8,128)(2,1)S(1)} %get-tuple-element.61), channel_id=1, source_target_pairs={{0,2},{1,3},{2,0},{3,1},{4,6},{5,7},{6,4},{7,5},{8,10},{9,11},{10,... | collective-permute-start | bytes 786440 | tf_op jit(solution)/shard_map/ppermute | solution.py:16
  68.3 27.4 %collective-permute-start.16 = (bf16[256,1024]{1,0:T(8,128)(2,1)S(1)}, bf16[256,1024]{1,0:T(8,128)(2,1)}, u32[]{:S(2)}, u32[]{:S(2)}) collective-permute-start(bf16[256,1024]{1,0:T(8,128)(2,1)S(1)} %shard_map.73), channel_id=1, source_target_pairs={{0,12},{1,13},{2,14},{3,15},{4,8},{5,9},{6,10},{7,11},{8,4},{9,5},... | collective-permute-start | bytes 1572872 | tf_op jit(solution)/shard_map/ppermute | solution.py:16
  71.6 6.8 %collective-permute-start.13 = (f32[8,128]{1,0:T(8,128)S(1)}, f32[8,128]{1,0:T(8,128)S(1)}, u32[]{:S(2)}, u32[]{:S(2)}) collective-permute-start(f32[8,128]{1,0:T(8,128)S(1)} %add.50), channel_id=1, source_target_pairs={{0,1},{1,0},{2,3},{3,2},{4,5},{5,4},{6,7},{7,6},{8,9},{9,8},{10,11... | collective-permute-start | bytes 12296 | tf_op jit(solution)/shard_map/ppermute | solution.py:16
  77.3 9.4 %collective-permute-start.20 = (bf16[128,1024]{1,0:T(8,128)(2,1)}, bf16[128,1024]{1,0:T(8,128)(2,1)}, u32[]{:S(2)}, u32[]{:S(2)}) collective-permute-start(bf16[128,1024]{1,0:T(8,128)(2,1)} %get-tuple-element.64), channel_id=1, source_target_pairs={{0,2},{1,3},{2,0},{3,1},{4,6},{5,7},{6,4},{7,5},{8,10},{9,11},{10,... | collective-permute-start | bytes 786440 | tf_op jit(solution)/shard_map/ppermute | solution.py:16
  78.4 11.8 %collective-permute-start.19 = (bf16[128,1024]{1,0:T(8,128)(2,1)}, bf16[128,1024]{1,0:T(8,128)(2,1)}, u32[]{:S(2)}, u32[]{:S(2)}) collective-permute-start(bf16[128,1024]{1,0:T(8,128)(2,1)} %shard_map.75), channel_id=1, source_target_pairs={{0,4},{1,5},{2,6},{3,7},{4,0},{5,1},{6,2},{7,3},{8,12},{9,13},{10,... | collective-permute-start | bytes 786440 | tf_op jit(solution)/shard_map/ppermute | solution.py:16
  82.9 12.8 %collective-permute-start.22 = (bf16[128,1024]{1,0:T(8,128)(2,1)}, bf16[128,1024]{1,0:T(8,128)(2,1)}, u32[]{:S(2)}, u32[]{:S(2)}) collective-permute-start(bf16[128,1024]{1,0:T(8,128)(2,1)} %shard_map.76), channel_id=1, source_target_pairs={{0,4},{1,5},{2,6},{3,7},{4,0},{5,1},{6,2},{7,3},{8,12},{9,13},{10,... | collective-permute-start | bytes 786440 | tf_op jit(solution)/shard_map/ppermute | solution.py:16

commit v3 on v2

--- a/solution.py
+++ b/solution.py
@@ -189,12 +189,36 @@
     return jnp.concatenate([pos, neg])
 
 
-def sum_kernel(groups, *refs):
+def add_kernel(starts, *refs):
+    *parts, out = refs
+    out[...] = sum(
+        part[start : start + out.shape[0], :].astype(jnp.float32) for start, part in zip(starts, parts)
+    ).astype(out.dtype)
+
+
+def add(rows, *parts):
+    vmem = pl.BlockSpec(memory_space=pltpu.VMEM)
+    width = parts[0][0].shape[1]
+    return pl.pallas_call(
+        functools.partial(add_kernel, [start for _, start in parts]),
+        in_specs=[vmem] * len(parts),
+        out_specs=vmem,
+        out_shape=pltpu.VMEM((rows, width), jnp.bfloat16),
+        cost_estimate=pl.CostEstimate(
+            flops=rows * width * len(parts), bytes_accessed=4 * rows * width, transcendentals=0
+        ),
+        compiler_params=pltpu.CompilerParams(vmem_limit_bytes=4 << 20),
+    )(*[pltpu.with_memory_space_constraint(part, pltpu.VMEM) for part, _ in parts])
+
+
+def finish_kernel(groups, n_loss, count, *refs):
     n_in = sum(len(group) for group in groups)
-    ins, outs, totals, sem = list(refs[:n_in]), refs[n_in : n_in + len(groups)], refs[n_in + len(groups) : -1], refs[-1]
+    losses, ins, refs = refs[:n_loss], list(refs[n_loss : n_loss + n_in]), refs[n_loss + n_in :]
+    loss_ref, outs, totals, sem = refs[0], refs[1 : 1 + len(groups)], refs[1 + len(groups) : -1], refs[-1]
     n, stores = 64, []
     for starts, out, total in zip(groups, outs, totals):
         parts = [(start, ins.pop(0)) for start in starts]
+        lanes = total.shape[2]
         for r in range(0, out.shape[0], n):
             here = pl.ds(r, n)
             value = sum(
@@ -202,48 +226,33 @@
                 for start, part in parts
                 if start <= r < start + part.shape[0]
             )
-            total[here] = value.reshape(n, *total.shape[1:])
+            for k in range(total.shape[1]):
+                total[here, k, :] = value[:, k * lanes : (k + 1) * lanes]
             stores.append(pltpu.make_async_copy(total.at[here], out.at[here], sem.at[len(stores)]))
             stores[-1].start()
+    loss_ref[0] = jnp.sum(sum(loss[...] for loss in losses)) * (1.0 / count)
     for copy in stores:
         copy.wait()
 
 
-def add_kernel(*refs):
-    *parts, out = refs
-    out[...] = sum(part[...].astype(jnp.float32) for part in parts).astype(out.dtype)
-
-
-def add(*parts):
-    vmem = pl.BlockSpec(memory_space=pltpu.VMEM)
-    return pl.pallas_call(
-        add_kernel,
-        in_specs=[vmem] * len(parts),
-        out_specs=vmem,
-        out_shape=pltpu.VMEM(parts[0].shape, jnp.bfloat16),
-        cost_estimate=pl.CostEstimate(
-            flops=parts[0].size * len(parts), bytes_accessed=4 * parts[0].size, transcendentals=0
+def finish_sums(groups, losses, length, count):
+    width, lanes = groups[0][0][1].shape[1], 128
+    smem, anywhere, vmem = (pl.BlockSpec(memory_space=m) for m in (pltpu.SMEM, pl.ANY, pltpu.VMEM))
+    flat = [*losses, *(part for group in groups for _, part in group)]
+    shape = (length, width // lanes, lanes)
+    loss, *outs = pl.pallas_call(
+        functools.partial(
+            finish_kernel, [[start for start, _ in group] for group in groups], len(losses), count
         ),
-        compiler_params=pltpu.CompilerParams(vmem_limit_bytes=4 << 20),
-    )(*[pltpu.with_memory_space_constraint(part, pltpu.VMEM) for part in parts])
-
-
-def finish_sums(groups, length):
-    width, lanes = groups[0][0][1].shape[1], 128
-    anywhere, vmem = pl.BlockSpec(memory_space=pl.ANY), pl.BlockSpec(memory_space=pltpu.VMEM)
-    flat = [part for group in groups for _, part in group]
-    shape = (length, width // lanes, lanes)
-    outs = pl.pallas_call(
-        functools.partial(sum_kernel, [[start for start, _ in group] for group in groups]),
         in_specs=[vmem] * len(flat),
-        out_specs=[anywhere] * len(groups),
-        out_shape=[jax.ShapeDtypeStruct(shape, jnp.float32)] * len(groups),
+        out_specs=[smem] + [anywhere] * len(groups),
+        out_shape=[jax.ShapeDtypeStruct((1,), jnp.float32)] + [jax.ShapeDtypeStruct(shape, jnp.float32)] * len(groups),
         scratch_shapes=[pltpu.VMEM(shape, jnp.float32)] * len(groups)
         + [pltpu.SemaphoreType.DMA((len(groups) * (length // 64),))],
         cost_estimate=pl.CostEstimate(flops=6 * length * width, bytes_accessed=20 * length * width, transcendentals=0),
         compiler_params=pltpu.CompilerParams(vmem_limit_bytes=16 << 20),
     )(*[pltpu.with_memory_space_constraint(x, pltpu.VMEM) for x in flat])
-    return [out.reshape(length, 1, width) for out in outs]
+    return [loss, *(out.reshape(length, 1, width) for out in outs)]
 
 
 def step(states, goals, pos_offset, neg_blocks):
@@ -257,76 +266,86 @@
         inner.append(bit)
         bit //= 2
     across = high ^ (high >> 1)
-    row_xors, col_xors = [0, 1, across, across ^ 1], subsets(inner)
+    blocks = subsets(inner)
+    n_block = len(blocks)
+    row_xors, col_xors = [0, across], [x ^ side for x in blocks for side in (0, 1)]
     n_row, n_col = len(row_xors) * length, len(col_xors) * length
-    last = n_col - length
+    last = n_col - 2 * length
     state, goal = states.reshape(length, width), goals.reshape(length, width)
     own = lax.axis_index(AXIS).astype(jnp.int32).reshape(1)
 
-    cols = {0: goal}
-    for bit in inner:
-        shift = len(cols) * length
-        cols = {**cols, **{p + shift: swap(c, bit, size) for p, c in cols.items()}}
-    sib = swap(state, 1, size)
-
-
     def outer(i):
         return (i & across) in (0, across)
 
+    mine = [goal]
+    for bit in inner:
+        mine = mine + [swap(block, bit, size) for block in mine]
+    side = [swap(block, 1, size) for block in mine]
+    cols = {2 * k * length + p: b for k in range(n_block) for p, b in ((0, mine[k]), (length, side[k]))}
     pair_in = swap(state, across, size, lambda i: not outer(i))
     pair = pair_in + swap(state, across, size, outer)
-    far = swap(pair, 1, size)
     table = counts(pos_offset, neg_blocks, size)
-    tables = [table] + [swap(table, x, size) for x in row_xors[1:]]
-
-    near, third = 2 * length, 3 * length
-    row_chunks = tuple((k * length, length, k, 0) for k in range(len(row_xors)))
-    col_chunks = tuple((k * length, length, k, 0) for k in range(len(col_xors)))
-    fixed = dict(row_chunks=row_chunks, col_chunks=col_chunks, row_xors=row_xors, col_xors=col_xors)
-    early = {p: c for p, c in cols.items() if 0 < p < last}
+    tables = [table, swap(table, across, size)]
+
+    fixed = dict(
+        row_xors=row_xors, col_xors=col_xors,
+        row_chunks=tuple((k * length, length, k, 0) for k in range(len(row_xors))),
+        col_chunks=tuple((k * length, length, k, 0) for k in range(len(col_xors))),
+    )
+
+    def arrived(start, end):
+        return {p: c for p, c in cols.items() if start <= p < end}
+
     loss_a, held, _, _ = phase(
-        own, tables[:2], {0: state, length: sib}, {0: goal}, None, new=[(0, near, 0, length)], **fixed
-    )
-    loss_b, held, _, _ = phase(own, tables[:2], {}, early, held, new=[(0, near, length, last)], **fixed)
-    loss_e, held, _, _ = phase(own, tables[:2], {}, {last: cols[last]}, held, new=[(0, near, last, n_col)], **fixed)
-    first = n_col // 2
-    soon_cols = [[(first, first + half)], [(first + half, first + length)]]
-    loss_c, held, _, soon = phase(
-        own, tables, {near: pair, third: far}, {}, held, new=[(near, n_row, 0, last)], col_outs=soon_cols, **fixed
-    )
-    loss_d, held, (far_part, pair_part), _ = phase(
-        own, tables, {}, {}, held, new=[(near, n_row, last, n_col)],
-        row_outs=[[(third, n_row)], [(near, third)]], **fixed,
-    )
-    loss = loss_a + loss_b + loss_c + loss_d + loss_e
-
-    back_far = swap(far_part, 1, size)
-    loss = loss + swap(loss, across, size)
-    back_pair = swap(add(pair_part, back_far), across, size)
-    sent_cols = [[(p, p + half)] for p in range(first + length, n_col, half)]
-    _, _, _, sent = phase(own, [], {}, {}, held, col_outs=sent_cols, **fixed)
-    parts = {out[0][0]: value for out, value in zip([*soon_cols, *sent_cols], [*soon, *sent])}
-    kept_cols = [[(0, length)]] + [[(p, p + half)] for p in range(length, n_col // 2, half)]
-    _, _, (own_part, sib_part), kept = phase(
-        own, [], {}, {}, held, row_outs=[[(0, length)], [(length, near)]], col_outs=kept_cols,
-        dtypes=[jnp.float32, jnp.bfloat16] + [jnp.float32] * len(kept_cols), **fixed,
-    )
-    parts.update({out[0][0]: value for out, value in zip(kept_cols, kept)})
-    back_sib = swap(sib_part, 1, size)
-    for k, bit in reversed(list(enumerate(inner))):
-        loss = loss + swap(loss, bit, size)
+        own, tables[:1], {0: state}, arrived(0, 2 * length), None, new=[(0, length, 0, 2 * length)], **fixed
+    )
+    loss_b, held, _, _ = phase(
+        own, tables[:1], {}, arrived(2 * length, last), held, new=[(0, length, 2 * length, last)], **fixed
+    )
+    loss_c, held, _, _ = phase(own, tables, {length: pair}, {}, held, new=[(length, n_row, 0, last)], **fixed)
+    sides, own_sums = {}, {}
+
+    def goal_phase(which, tables, cols, held, new, rows=()):
+        pieces = [[(p * length, (p + 1) * length)] for k in which for p in (2 * k + 1, 2 * k)]
+        loss, held, row_outs, outs = phase(
+            own, tables, {}, cols, held, new=new, row_outs=rows, col_outs=pieces,
+            dtypes=[jnp.float32] * len(rows) + [jnp.bfloat16, jnp.float32] * len(which), **fixed,
+        )
+        sides.update(zip(which, outs[0::2]))
+        own_sums.update(zip(which, outs[1::2]))
+        return loss, held, row_outs
+
+    top = n_block // 2
+    loss_d, held, _ = goal_phase(
+        list(range(n_block - 1, top, -1)), tables, arrived(last, n_col), held, [(0, n_row, last, n_col)]
+    )
+    loss = loss_a + loss_b + loss_c + loss_d
     loss = loss + swap(loss, 1, size)
-    got = {}
-    for k in reversed(range(len(inner))):
-        lower = length << k
-        for p in sorted(p - lower for p in parts if p >= lower)[::-1]:
-            mine = parts.pop(p + lower)
-            if p + lower in got:
-                mine = add(mine, *got.pop(p + lower))
-            got.setdefault(p, []).append(swap(mine, inner[k], size))
-    goal_parts = [(0, parts[0])] + [(p, part) for p, received in got.items() for part in received]
-    grad_states, grad_goals = finish_sums([[(0, own_part), (0, back_sib), (0, back_pair)], goal_parts], length)
-    loss_mean = jnp.sum(loss).reshape(1) / (size * length)
+    _, _, (pair_part,), _ = phase(own, [], {}, {}, held, row_outs=[[(length, n_row)]], **fixed)
+
+    back_pair = swap(pair_part, across, size)
+    goal_phase([top], [], {}, held, ())
+    _, _, (own_part,) = goal_phase(list(range(top)), [], {}, held, (), rows=[[(0, length)]])
+    cross = {k: swap(part, 1, size) for k, part in sides.items()}
+    for s in reversed(range(len(inner))):
+        loss = loss + swap(loss, inner[s], size)
+    losses = [loss, swap(loss, across, size)]
+    addends = {k: [(own_sums[k], 0), (cross[k], 0)] for k in range(n_block)}
+    halves = {(k, o): [] for k in range(n_block) for o in (0, half)}
+    for s in reversed(range(len(inner))):
+        for k in reversed(range(1 << s, 2 << s)):
+            to = k - (1 << s)
+            if to == 0 and s == len(inner) - 1:
+                whole = add(length, *addends[k])
+                addends[to].append((swap(whole, inner[s], size), 0))
+                continue
+            for o in (0, half):
+                piece = add(half, *[(b, o) for b, _ in addends[k]], *[(b, 0) for b in halves[k, o]])
+                halves[to, o].append(swap(piece, inner[s], size))
+    goal_parts = [(0, block) for block, _ in addends[0]] + [(o, b) for o in (0, half) for b in halves[0, o]]
+    loss_mean, grad_states, grad_goals = finish_sums(
+        [[(0, own_part), (0, back_pair)], goal_parts], losses, length, size * length
+    )
     return (loss_mean, grad_states, grad_goals)
 
 

time: 99.9 us -> 96.6 us (0.967)
  starting transfers between devices: 22 us -> 32.3 us
  waiting for transfers between devices: 50.7 us -> 42.9 us
  Pallas kernels: 19.8 us -> 16.4 us
  between operations: 2.6 us -> 0.84 us
    ppermute x23 -> x24, starting transfers between devices: 22 us -> 32.3 us  [swap(): lax.ppermute(value, AXIS, [(i, i ^ offset) for i in range(size) if only(i)])]
    ppermute x23 -> x24, waiting for transfers between devices: 50.7 us -> 42.9 us  [swap(): lax.ppermute(value, AXIS, [(i, i ^ offset) for i in range(size) if only(i)])]
    pallas_call x7, Pallas kernels: 15.5 us -> 13.3 us  [phase(): pl.pallas_call(functools.partial(tile_kernel, plan), in_specs=in_specs, o...]
    pallas_call x4 -> x6, Pallas kernels: 4.32 us -> 3.18 us  [the longest x1 2.81 us: finish_sums(): pl.pallas_call(functools.partial(finish_kernel, [[start for start, _ in g...]
  transfers between devices with their start and end apart: 23 -> 24, of which waited for: 12 -> 10; matrix products, arithmetic and copies ran while one was open for 2% -> 2% of each run, Pallas kernels for 10% -> 11%
where the time goes in v3:
time: 96.6 us; the launch traced here: 96.3 us
  waiting for transfers between devices  42.9 us (44%)
  starting transfers between devices  32.3 us (33%)
  Pallas kernels  16.4 us (17%)
  local copies, waits for them, and re-layouts  2.08 us (2%)
  other arithmetic  1.77 us (2%)
    ppermute x24, waiting for transfers between devices, swap(): lax.ppermute(value, AXIS, [(i, i ^ offset) for i in range(size) if only(i)])  42.9 us
    ppermute x24, starting transfers between devices, swap(): lax.ppermute(value, AXIS, [(i, i ^ offset) for i in range(size) if only(i)])  32.3 us
    pallas_call x7, Pallas kernels, phase(): pl.pallas_call(functools.partial(tile_kernel, plan), in_specs=in_specs, o...  13.3 us
    pallas_call x1, Pallas kernels, finish_sums(): pl.pallas_call(functools.partial(finish_kernel, [[start for start, _ in g...  2.81 us
    unnamed x4, local copies, waits for them, and re-layouts  2.08 us
  transfers between devices with their start and end apart: 24, of which 10 were waited for; matrix products, arithmetic and copies ran while one was open for 2% of the time, Pallas kernels for 11%

profile of v3, /device:TPU:0, one launch (start us, length us, event | category | flops | bytes accessed | tf_op | source)
XLA Modules:
  0.0 96.3 jit_solution(4515270111937293846)
XLA Ops:
  0.6 3.1 %collective-permute-start.1 = (bf16[256,1024]{1,0:T(8,128)(2,1)}, bf16[256,1024]{1,0:T(8,128)(2,1)S(1)}, u32[]{:S(2)}, u32[]{:S(2)}) collective-permute-start(bf16[256,1024]{1,0:T(8,128)(2,1)} %bitcast.8), channel_id=1, source_target_pairs={{0,4},{1,5},{2,6},{3,7},{4,0},{5,1},{6,2},{7,3},{8,12},{9,13},{10,... | collective-permute-start | bytes 1572872 | tf_op jit(solution)/shard_map/ppermute | solution.py:16
  3.7 1.5 %collective-permute-start.3 = (bf16[256,1024]{1,0:T(8,128)(2,1)}, bf16[256,1024]{1,0:T(8,128)(2,1)S(1)}, u32[]{:S(2)}, u32[]{:S(2)}) collective-permute-start(bf16[256,1024]{1,0:T(8,128)(2,1)} %bitcast.9), channel_id=1, source_target_pairs={{0,2},{1,3},{2,0},{3,1},{4,6},{5,7},{6,4},{7,5},{8,10},{9,11},{10,... | collective-permute-start | bytes 1572872 | tf_op jit(solution)/shard_map/ppermute | solution.py:16
  5.3 0.7 collective-permute-start.6
  6.0 9.9 %collective-permute-done.1.refs_1_ = bf16[256,1024]{1,0:T(8,128)(2,1)S(1)} collective-permute-done((bf16[256,1024]{1,0:T(8,128)(2,1)}, bf16[256,1024]{1,0:T(8,128)(2,1)S(1)}, u32[]{:S(2)}, u32[]{:S(2)}) %collective-permute-start.1) | collective-permute-done | bytes 524320 | tf_op jit(solution)/shard_map/ppermute | solution.py:16
  15.9 1.7 %collective-permute-start.8 = (bf16[256,1024]{1,0:T(8,128)(2,1)S(1)}, bf16[256,1024]{1,0:T(8,128)(2,1)S(1)}, u32[]{:S(2)}, u32[]{:S(2)}) collective-permute-start(bf16[256,1024]{1,0:T(8,128)(2,1)S(1)} %collective-permute-done.1.refs_1_), channel_id=1, source_target_pairs={{0,2},{1,3},{2,0},{3,1},{4,6},{5,7},{6,4},{7,5},{8,10},{9,11},{10,... | collective-permute-start | bytes 1572872 | tf_op jit(solution)/shard_map/ppermute | solution.py:16
  17.6 5.5 %collective-permute-start.7 = (bf16[256,1024]{1,0:T(8,128)(2,1)}, bf16[256,1024]{1,0:T(8,128)(2,1)S(1)}, u32[]{:S(2)}, u32[]{:S(2)}) collective-permute-start(bf16[256,1024]{1,0:T(8,128)(2,1)} %bitcast.13), channel_id=1, source_target_pairs={{0,12},{1,13},{2,14},{3,15},{12,0},{13,1},{14,2},{15,3},{16,28},{1... | collective-permute-start | bytes 1572872 | tf_op jit(solution)/shard_map/ppermute | solution.py:16
  23.1 0.3 collective-permute-start.2
  23.4 0.3 collective-permute-start.4
  23.7 5.3 %collective-permute-done.8.refs_2_ = bf16[256,1024]{1,0:T(8,128)(2,1)S(1)} collective-permute-done((bf16[256,1024]{1,0:T(8,128)(2,1)S(1)}, bf16[256,1024]{1,0:T(8,128)(2,1)S(1)}, u32[]{:S(2)}, u32[]{:S(2)}) %collective-permute-start.8) | collective-permute-done | bytes 524320 | tf_op jit(solution)/shard_map/ppermute | solution.py:16
  29.0 0.7 add_bitcast_fusion
  29.6 0.1 convert_reduce_fusion.1
  29.7 0.7 convert_reduce_fusion
  30.5 0.1 pad_maximum_fusion.refs_0_
  30.5 5.3 %collective-permute-done.7 = bf16[256,1024]{1,0:T(8,128)(2,1)S(1)} collective-permute-done((bf16[256,1024]{1,0:T(8,128)(2,1)}, bf16[256,1024]{1,0:T(8,128)(2,1)S(1)}, u32[]{:S(2)}, u32[]{:S(2)}) %collective-permute-start.7) | collective-permute-done | bytes 524320 | tf_op jit(solution)/shard_map/ppermute | solution.py:16
  35.9 3.5 %collective-permute-start.5 = (f32[32]{0:T(128)S(1)}, f32[32]{0:T(128)S(1)}, u32[]{:S(2)}, u32[]{:S(2)}) collective-permute-start(f32[32]{0:T(128)S(1)} %pad_maximum_fusion.refs_0_), channel_id=1, source_target_pairs={{0,12},{1,13},{2,14},{3,15},{4,8},{5,9},{6,10},{7,11},{8,4},{9,5},... | collective-permute-start | bytes 392 | tf_op jit(solution)/shard_map/ppermute | solution.py:16
  39.4 0.2 add.38.refs_2_
  39.6 0.0 copy-start
  39.6 1.0 %copy-done = bf16[256,1,1024]{2,0,1:T(8,128)(2,1)S(1)} copy-done((bf16[256,1,1024]{2,0,1:T(8,128)(2,1)S(1)}, bf16[256,1,1024]{2,0,1:T(8,128)(2,1)}, u32[]{:S(2)}) %copy-start) | copy-done | bytes 524312
  40.7 1.0 %copy-done.1 = bf16[256,1,1024]{2,0,1:T(8,128)(2,1)S(1)} copy-done((bf16[256,1,1024]{2,0,1:T(8,128)(2,1)S(1)}, bf16[256,1,1024]{2,0,1:T(8,128)(2,1)}, u32[]{:S(2)}) %copy-start.1) | copy-done | bytes 524312
  41.7 1.5 %shard_map.67 = (f32[8,128]{1,0:T(8,128)S(1)}, bf16[512,1024]{1,0:T(8,128)(2,1)S(1)}, bf16[2048,1024]{1,0:T(8,128)(2,1)S(1)}, bf16[512,2048]{1,0:T(8,128)(2,1)S(1)}) custom-call(s32[1]{0:T(128)} %bitcast.own_ref, f32[32]{0:T(128)S(1)} %pad_maximum_fusion.refs_0_, bf16[256,1024]{1,0:T(8,128)(2,1)S(1)} %bitcast.14, bf16[256,1024]{1,0:T(8,128)(2,1)S(1)} %bitcast.11, ...), custom_call_target="tpu_custom_call" | custom-call | flops 268435456 | bytes 4194304 | tf_op jit(solution)/shard_map/pallas_call | solution.py:161
  43.3 2.1 %shard_map.68 = (f32[8,128]{1,0:T(8,128)S(1)}, bf16[512,1024]{1,0:T(8,128)(2,1)S(1)}, bf16[2048,1024]{1,0:T(8,128)(2,1)S(1)}, bf16[512,2048]{1,0:T(8,128)(2,1)S(1)}) custom-call(s32[1]{0:T(128)} %bitcast.own_ref, f32[32]{0:T(128)S(1)} %pad_maximum_fusion.refs_0_, ...), custom_call_target="tpu_custom_call", output_to_operand_aliasing={{1}: (6, {}), {2}: (7, {}), {3}: (8, {})} | custom-call | flops 536870912 | bytes 4194304 | tf_op jit(solution)/shard_map/pallas_call | solution.py:161
  45.4 2.5 %shard_map.69 = (f32[8,128]{1,0:T(8,128)S(1)}, bf16[512,1024]{1,0:T(8,128)(2,1)S(1)}, bf16[2048,1024]{1,0:T(8,128)(2,1)S(1)}, bf16[512,2048]{1,0:T(8,128)(2,1)S(1)}) custom-call(s32[1]{0:T(128)} %bitcast.own_ref, f32[32]{0:T(128)S(1)} %pad_maximum_fusion.refs_0_, ...), custom_call_target="tpu_custom_call", output_to_operand_aliasing={{1}: (4, {}), {2}: (5, {}), {3}: (6, {})} | custom-call | flops 805306368 | bytes 4194304 | tf_op jit(solution)/shard_map/pallas_call | solution.py:161
  47.9 2.7 %shard_map.70 = (f32[8,128]{1,0:T(8,128)S(1)}, bf16[512,1024]{1,0:T(8,128)(2,1)S(1)}, bf16[2048,1024]{1,0:T(8,128)(2,1)S(1)}, bf16[512,2048]{1,0:T(8,128)(2,1)S(...) custom-call(s32[1]{0:T(128)} %bitcast.own_ref, ...), custom_call_target="tpu_custom_call", output_to_operand_aliasing={{1}: (5, {}), {2}: (6, {}), {3}: (7, {})} | custom-call | flops 1073741824 | bytes 4194304 | tf_op jit(solution)/shard_map/pallas_call | solution.py:161
  50.6 0.1 collective-permute-start.19
  50.7 0.8 shard_map.73
  51.5 0.6 collective-permute-start.16
  52.0 2.4 %shard_map.71 = (f32[256,1024]{1,0:T(8,128)S(1)}, bf16[256,1024]{1,0:T(8,128)(2,1)S(1)}, f32[256,1024]{1,0:T(8,128)S(1)}, bf16[256,1024]{1,0:T(8,128)(2,1)S(1)}, f32[256,1024]{1,0:T(8,128)S(1)}) custom-call(s32[1]{0:T(128)} %bitcast.own_ref, bf16[512,1024]{1,0:T(8,128)(2,1)S(1)} %get-tuple-element.44.refs_0_, ...), custom_call_target="tpu_custom_call" | custom-call | flops 2147483648 | bytes 4194304 | tf_op jit(solution)/shard_map/pallas_call | solution.py:161
  54.4 0.1 collective-permute-start.18
  54.5 0.5 collective-permute-start.10
  55.0 1.4 %collective-permute-done.10 = f32[8,128]{1,0:T(8,128)S(1)} collective-permute-done((f32[8,128]{1,0:T(8,128)S(1)}, f32[8,128]{1,0:T(8,128)S(1)}, u32[]{:S(2)}, u32[]{:S(2)}) %collective-permute-start.10) | collective-permute-done | bytes 4128 | tf_op jit(solution)/shard_map/ppermute | solution.py:16
  56.4 0.5 collective-permute-start.11
  56.9 3.1 %collective-permute-done.11 = f32[8,128]{1,0:T(8,128)S(1)} collective-permute-done((f32[8,128]{1,0:T(8,128)S(1)}, f32[8,128]{1,0:T(8,128)S(1)}, u32[]{:S(2)}, u32[]{:S(2)}) %collective-permute-start.11) | collective-permute-done | bytes 4128 | tf_op jit(solution)/shard_map/ppermute | solution.py:16
  60.1 0.6 collective-permute-start.22
  60.6 1.3 %shard_map.72 = bf16[256,1024]{1,0:T(8,128)(2,1)S(1)} custom-call(s32[1]{0:T(128)} %bitcast.own_ref, bf16[512,1024]{1,0:T(8,128)(2,1)S(1)} %get-tuple-element.44.refs_0_, bf16[2048,1024]{1,0:T(8,128)(2,1)S(1)} %get-tuple-element.45.refs_1_, bf16[512,2048]{1,0:T(8,128)(2,1)S(1)} %get-tuple-element.46.refs_2_), custom_call_target="tpu_custom_call" | custom-call | flops 1073741824 | bytes 4194304 | tf_op jit(solution)/shard_map/pallas_call | solution.py:161
  61.9 0.3 collective-permute-start.14
  62.3 1.3 %collective-permute-done.12 = f32[8,128]{1,0:T(8,128)S(1)} collective-permute-done((f32[8,128]{1,0:T(8,128)S(1)}, f32[8,128]{1,0:T(8,128)S(1)}, u32[]{:S(2)}, u32[]{:S(2)}) %collective-permute-start.12) | collective-permute-done | bytes 4128 | tf_op jit(solution)/shard_map/ppermute | solution.py:16
  63.6 0.5 collective-permute-start.20
  64.1 0.1 shard_map.74
  64.2 1.6 %collective-permute-start.17 = (bf16[256,1024]{1,0:T(8,128)(2,1)S(1)}, bf16[256,1024]{1,0:T(8,128)(2,1)S(1)}, u32[]{:S(2)}, u32[]{:S(2)}) collective-permute-start(bf16[256,1024]{1,0:T(8,128)(2,1)S(1)} %shard_map.74), channel_id=1, source_target_pairs={{0,2},{1,3},{2,0},{3,1},{4,6},{5,7},{6,4},{7,5},{8,10},{9,11},{10,... | collective-permute-start | bytes 1572872 | tf_op jit(solution)/shard_map/ppermute | solution.py:16
  65.8 3.5 %collective-permute-done.22.refs_2_ = bf16[128,1024]{1,0:T(8,128)(2,1)S(1)} collective-permute-done((bf16[128,1024]{1,0:T(8,128)(2,1)S(1)}, bf16[128,1024]{1,0:T(8,128)(2,1)S(1)}, u32[]{:S(2)}, u32[]{:S(2)}) %collective-permute-start.22) | collective-permute-done | bytes 262176 | tf_op jit(solution)/shard_map/ppermute | solution.py:16
  69.3 0.1 shard_map.78
  69.4 5.5 %collective-permute-done.20.refs_2_ = bf16[128,1024]{1,0:T(8,128)(2,1)S(1)} collective-permute-done((bf16[128,1024]{1,0:T(8,128)(2,1)S(1)}, bf16[128,1024]{1,0:T(8,128)(2,1)S(1)}, u32[]{:S(2)}, u32[]{:S(2)}) %collective-permute-start.20) | collective-permute-done | bytes 262176 | tf_op jit(solution)/shard_map/ppermute | solution.py:16
  74.9 2.0 %collective-permute-start.23 = (bf16[128,1024]{1,0:T(8,128)(2,1)S(1)}, bf16[128,1024]{1,0:T(8,128)(2,1)S(1)}, u32[]{:S(2)}, u32[]{:S(2)}) collective-permute-start(bf16[128,1024]{1,0:T(8,128)(2,1)S(1)} %shard_map.78), channel_id=1, source_target_pairs={{0,4},{1,5},{2,6},{3,7},{4,0},{5,1},{6,2},{7,3},{8,12},{9,13},{10,... | collective-permute-start | bytes 786440 | tf_op jit(solution)/shard_map/ppermute | solution.py:16
  77.0 0.1 shard_map.76
  77.1 1.6 %collective-permute-done.13.refs_1_ = f32[8,128]{1,0:T(8,128)S(1)} collective-permute-done((f32[8,128]{1,0:T(8,128)S(1)}, f32[8,128]{1,0:T(8,128)S(1)}, u32[]{:S(2)}, u32[]{:S(2)}) %collective-permute-start.13) | collective-permute-done | bytes 4128 | tf_op jit(solution)/shard_map/ppermute | solution.py:16
  78.7 9.0 %collective-permute-start.21 = (bf16[128,1024]{1,0:T(8,128)(2,1)S(1)}, bf16[128,1024]{1,0:T(8,128)(2,1)S(1)}, u32[]{:S(2)}, u32[]{:S(2)}) collective-permute-start(bf16[128,1024]{1,0:T(8,128)(2,1)S(1)} %shard_map.76), channel_id=1, source_target_pairs={{0,4},{1,5},{2,6},{3,7},{4,0},{5,1},{6,2},{7,3},{8,12},{9,13},{10,... | collective-permute-start | bytes 786440 | tf_op jit(solution)/shard_map/ppermute | solution.py:16
  87.7 5.8 %collective-permute-done.21.refs_7_ = bf16[128,1024]{1,0:T(8,128)(2,1)S(1)} collective-permute-done((bf16[128,1024]{1,0:T(8,128)(2,1)S(1)}, bf16[128,1024]{1,0:T(8,128)(2,1)S(1)}, u32[]{:S(2)}, u32[]{:S(2)}) %collective-permute-start.21) | collective-permute-done | bytes 262176 | tf_op jit(solution)/shard_map/ppermute | solution.py:16
  93.5 2.8 %shard_map.79 = (f32[1]{0:T(128)}, f32[256,8,128]{2,1,0:T(8,128)}, f32[256,8,128]{2,1,0:T(8,128)}) custom-call(f32[8,128]{1,0:T(8,128)S(1)} %add.43.refs_0_, f32[8,128]{1,0:T(8,128)S(1)} %collective-permute-done.13.refs_1_, f32[256,1024]{1,0:T(8,128)S(1)} %get-tuple-element.47.refs_2_, bf16[256,1024]{1,0:T(8,128)(2,1)S(1)} %collective-permute-done.14.refs_3_, ...), custom_call_target="tpu_custom_call" | custom-call | flops 1572864 | bytes 5242880 | tf_op jit(solution)/shard_map/pallas_call | solution.py:243
  (26 shorter events, 0.2 us)
Async XLA Ops:
  0.6 15.3 %collective-permute-start.1 = (bf16[256,1024]{1,0:T(8,128)(2,1)}, bf16[256,1024]{1,0:T(8,128)(2,1)S(1)}, u32[]{:S(2)}, u32[]{:S(2)}) collective-permute-start(bf16[256,1024]{1,0:T(8,128)(2,1)} %bitcast.8), channel_id=1, source_target_pairs={{0,4},{1,5},{2,6},{3,7},{4,0},{5,1},{6,2},{7,3},{8,12},{9,13},{10,... | collective-permute-start | bytes 1572872 | tf_op jit(solution)/shard_map/ppermute | solution.py:16
  3.7 19.3 %collective-permute-start.3 = (bf16[256,1024]{1,0:T(8,128)(2,1)}, bf16[256,1024]{1,0:T(8,128)(2,1)S(1)}, u32[]{:S(2)}, u32[]{:S(2)}) collective-permute-start(bf16[256,1024]{1,0:T(8,128)(2,1)} %bitcast.9), channel_id=1, source_target_pairs={{0,2},{1,3},{2,0},{3,1},{4,6},{5,7},{6,4},{7,5},{8,10},{9,11},{10,... | collective-permute-start | bytes 1572872 | tf_op jit(solution)/shard_map/ppermute | solution.py:16
  5.3 18.1 %collective-permute-start.6 = (bf16[256,1024]{1,0:T(8,128)(2,1)}, bf16[256,1024]{1,0:T(8,128)(2,1)S(1)}, u32[]{:S(2)}, u32[]{:S(2)}) collective-permute-start(bf16[256,1024]{1,0:T(8,128)(2,1)} %bitcast.12), channel_id=1, source_target_pairs={{4,8},{5,9},{6,10},{7,11},{8,4},{9,5},{10,6},{11,7},{20,24},{21,25... | collective-permute-start | bytes 1572872 | tf_op jit(solution)/shard_map/ppermute | solution.py:16
  15.9 13.1 %collective-permute-start.8 = (bf16[256,1024]{1,0:T(8,128)(2,1)S(1)}, bf16[256,1024]{1,0:T(8,128)(2,1)S(1)}, u32[]{:S(2)}, u32[]{:S(2)}) collective-permute-start(bf16[256,1024]{1,0:T(8,128)(2,1)S(1)} %collective-permute-done.1.refs_1_), channel_id=1, source_target_pairs={{0,2},{1,3},{2,0},{3,1},{4,6},{5,7},{6,4},{7,5},{8,10},{9,11},{10,... | collective-permute-start | bytes 1572872 | tf_op jit(solution)/shard_map/ppermute | solution.py:16
  17.6 22.0 %collective-permute-start = (bf16[256,1024]{1,0:T(8,128)(2,1)}, bf16[256,1024]{1,0:T(8,128)(2,1)S(1)}, u32[]{:S(2)}, u32[]{:S(2)}) collective-permute-start(bf16[256,1024]{1,0:T(8,128)(2,1)} %bitcast.10), channel_id=1, source_target_pairs={{0,1},{1,0},{2,3},{3,2},{4,5},{5,4},{6,7},{7,6},{8,9},{9,8},{10,11... | collective-permute-start | bytes 1572872 | tf_op jit(solution)/shard_map/ppermute | solution.py:16
  17.6 18.3 %collective-permute-start.7 = (bf16[256,1024]{1,0:T(8,128)(2,1)}, bf16[256,1024]{1,0:T(8,128)(2,1)S(1)}, u32[]{:S(2)}, u32[]{:S(2)}) collective-permute-start(bf16[256,1024]{1,0:T(8,128)(2,1)} %bitcast.13), channel_id=1, source_target_pairs={{0,12},{1,13},{2,14},{3,15},{12,0},{13,1},{14,2},{15,3},{16,28},{1... | collective-permute-start | bytes 1572872 | tf_op jit(solution)/shard_map/ppermute | solution.py:16
  23.1 20.1 %collective-permute-start.2 = (bf16[256,1024]{1,0:T(8,128)(2,1)S(1)}, bf16[256,1024]{1,0:T(8,128)(2,1)S(1)}, u32[]{:S(2)}, u32[]{:S(2)}) collective-permute-start(bf16[256,1024]{1,0:T(8,128)(2,1)S(1)} %collective-permute-done.1.refs_1_), channel_id=1, source_target_pairs={{0,1},{1,0},{2,3},{3,2},{4,5},{5,4},{6,7},{7,6},{8,9},{9,8},{10,11... | collective-permute-start | bytes 1572872 | tf_op jit(solution)/shard_map/ppermute | solution.py:16
  23.4 19.9 %collective-permute-start.4 = (bf16[256,1024]{1,0:T(8,128)(2,1)S(1)}, bf16[256,1024]{1,0:T(8,128)(2,1)S(1)}, u32[]{:S(2)}, u32[]{:S(2)}) collective-permute-start(bf16[256,1024]{1,0:T(8,128)(2,1)S(1)} %collective-permute-done.3.refs_3_), channel_id=1, source_target_pairs={{0,1},{1,0},{2,3},{3,2},{4,5},{5,4},{6,7},{7,6},{8,9},{9,8},{10,11... | collective-permute-start | bytes 1572872 | tf_op jit(solution)/shard_map/ppermute | solution.py:16
  29.0 18.9 %collective-permute-start.9 = (bf16[256,1024]{1,0:T(8,128)(2,1)S(1)}, bf16[256,1024]{1,0:T(8,128)(2,1)S(1)}, u32[]{:S(2)}, u32[]{:S(2)}) collective-permute-start(bf16[256,1024]{1,0:T(8,128)(2,1)S(1)} %collective-permute-done.8.refs_2_), channel_id=1, source_target_pairs={{0,1},{1,0},{2,3},{3,2},{4,5},{5,4},{6,7},{7,6},{8,9},{9,8},{10,11... | collective-permute-start | bytes 1572872 | tf_op jit(solution)/shard_map/ppermute | solution.py:16
  35.9 9.5 %collective-permute-start.5 = (f32[32]{0:T(128)S(1)}, f32[32]{0:T(128)S(1)}, u32[]{:S(2)}, u32[]{:S(2)}) collective-permute-start(f32[32]{0:T(128)S(1)} %pad_maximum_fusion.refs_0_), channel_id=1, source_target_pairs={{0,12},{1,13},{2,14},{3,15},{4,8},{5,9},{6,10},{7,11},{8,4},{9,5},... | collective-permute-start | bytes 392 | tf_op jit(solution)/shard_map/ppermute | solution.py:16
  39.6 1.0 %copy-start = (bf16[256,1,1024]{2,0,1:T(8,128)(2,1)S(1)}, bf16[256,1,1024]{2,0,1:T(8,128)(2,1)}, u32[]{:S(2)}) copy-start(bf16[256,1,1024]{2,0,1:T(8,128)(2,1)} %param.5) | copy-start | bytes 1572868
  40.7 1.0 %copy-start.1 = (bf16[256,1,1024]{2,0,1:T(8,128)(2,1)S(1)}, bf16[256,1,1024]{2,0,1:T(8,128)(2,1)}, u32[]{:S(2)}) copy-start(bf16[256,1,1024]{2,0,1:T(8,128)(2,1)} %param.4) | copy-start | bytes 1572868
  50.6 9.4 %collective-permute-start.19 = (bf16[256,1024]{1,0:T(8,128)(2,1)S(1)}, bf16[256,1024]{1,0:T(8,128)(2,1)S(1)}, u32[]{:S(2)}, u32[]{:S(2)}) collective-permute-start(bf16[256,1024]{1,0:T(8,128)(2,1)S(1)} %get-tuple-element.55), channel_id=1, source_target_pairs={{0,1},{1,0},{2,3},{3,2},{4,5},{5,4},{6,7},{7,6},{8,9},{9,8},{10,11... | collective-permute-start | bytes 1572872 | tf_op jit(solution)/shard_map/ppermute | solution.py:16
  51.5 12.7 %collective-permute-start.16 = (bf16[256,1024]{1,0:T(8,128)(2,1)S(1)}, bf16[256,1024]{1,0:T(8,128)(2,1)S(1)}, u32[]{:S(2)}, u32[]{:S(2)}) collective-permute-start(bf16[256,1024]{1,0:T(8,128)(2,1)S(1)} %get-tuple-element.51), channel_id=1, source_target_pairs={{0,1},{1,0},{2,3},{3,2},{4,5},{5,4},{6,7},{7,6},{8,9},{9,8},{10,11... | collective-permute-start | bytes 1572872 | tf_op jit(solution)/shard_map/ppermute | solution.py:16
  54.4 9.8 %collective-permute-start.18 = (bf16[256,1024]{1,0:T(8,128)(2,1)S(1)}, bf16[256,1024]{1,0:T(8,128)(2,1)S(1)}, u32[]{:S(2)}, u32[]{:S(2)}) collective-permute-start(bf16[256,1024]{1,0:T(8,128)(2,1)S(1)} %get-tuple-element.53), channel_id=1, source_target_pairs={{0,1},{1,0},{2,3},{3,2},{4,5},{5,4},{6,7},{7,6},{8,9},{9,8},{10,11... | collective-permute-start | bytes 1572872 | tf_op jit(solution)/shard_map/ppermute | solution.py:16
  54.5 1.9 %collective-permute-start.10 = (f32[8,128]{1,0:T(8,128)S(1)}, f32[8,128]{1,0:T(8,128)S(1)}, u32[]{:S(2)}, u32[]{:S(2)}) collective-permute-start(f32[8,128]{1,0:T(8,128)S(1)} %add_add_fusion), channel_id=1, source_target_pairs={{0,1},{1,0},{2,3},{3,2},{4,5},{5,4},{6,7},{7,6},{8,9},{9,8},{10,11... | collective-permute-start | bytes 12296 | tf_op jit(solution)/shard_map/ppermute | solution.py:16
  56.4 3.6 %collective-permute-start.11 = (f32[8,128]{1,0:T(8,128)S(1)}, f32[8,128]{1,0:T(8,128)S(1)}, u32[]{:S(2)}, u32[]{:S(2)}) collective-permute-start(f32[8,128]{1,0:T(8,128)S(1)} %add.41), channel_id=1, source_target_pairs={{0,2},{1,3},{2,0},{3,1},{4,6},{5,7},{6,4},{7,5},{8,10},{9,11},{10,... | collective-permute-start | bytes 12296 | tf_op jit(solution)/shard_map/ppermute | solution.py:16
  60.0 3.6 %collective-permute-start.12 = (f32[8,128]{1,0:T(8,128)S(1)}, f32[8,128]{1,0:T(8,128)S(1)}, u32[]{:S(2)}, u32[]{:S(2)}) collective-permute-start(f32[8,128]{1,0:T(8,128)S(1)} %add.42), channel_id=1, source_target_pairs={{0,4},{1,5},{2,6},{3,7},{4,0},{5,1},{6,2},{7,3},{8,12},{9,13},{10,... | collective-permute-start | bytes 12296 | tf_op jit(solution)/shard_map/ppermute | solution.py:16
  60.1 9.2 %collective-permute-start.22 = (bf16[128,1024]{1,0:T(8,128)(2,1)S(1)}, bf16[128,1024]{1,0:T(8,128)(2,1)S(1)}, u32[]{:S(2)}, u32[]{:S(2)}) collective-permute-start(bf16[128,1024]{1,0:T(8,128)(2,1)S(1)} %shard_map.77), channel_id=1, source_target_pairs={{0,2},{1,3},{2,0},{3,1},{4,6},{5,7},{6,4},{7,5},{8,10},{9,11},{10,... | collective-permute-start | bytes 786440 | tf_op jit(solution)/shard_map/ppermute | solution.py:16
  61.9 25.8 %collective-permute-start.14 = (bf16[256,1024]{1,0:T(8,128)(2,1)S(1)}, bf16[256,1024]{1,0:T(8,128)(2,1)S(1)}, u32[]{:S(2)}, u32[]{:S(2)}) collective-permute-start(bf16[256,1024]{1,0:T(8,128)(2,1)S(1)} %shard_map.72), channel_id=1, source_target_pairs={{0,12},{1,13},{2,14},{3,15},{4,8},{5,9},{6,10},{7,11},{8,4},{9,5},... | collective-permute-start | bytes 1572872 | tf_op jit(solution)/shard_map/ppermute | solution.py:16
  63.6 11.3 %collective-permute-start.20 = (bf16[128,1024]{1,0:T(8,128)(2,1)S(1)}, bf16[128,1024]{1,0:T(8,128)(2,1)S(1)}, u32[]{:S(2)}, u32[]{:S(2)}) collective-permute-start(bf16[128,1024]{1,0:T(8,128)(2,1)S(1)} %shard_map.75), channel_id=1, source_target_pairs={{0,2},{1,3},{2,0},{3,1},{4,6},{5,7},{6,4},{7,5},{8,10},{9,11},{10,... | collective-permute-start | bytes 786440 | tf_op jit(solution)/shard_map/ppermute | solution.py:16
  64.1 23.6 %collective-permute-start.15 = (bf16[256,1024]{1,0:T(8,128)(2,1)S(1)}, bf16[256,1024]{1,0:T(8,128)(2,1)S(1)}, u32[]{:S(2)}, u32[]{:S(2)}) collective-permute-start(bf16[256,1024]{1,0:T(8,128)(2,1)S(1)} %get-tuple-element.49), channel_id=1, source_target_pairs={{0,1},{1,0},{2,3},{3,2},{4,5},{5,4},{6,7},{7,6},{8,9},{9,8},{10,11... | collective-permute-start | bytes 1572872 | tf_op jit(solution)/shard_map/ppermute | solution.py:16
  64.2 29.3 %collective-permute-start.17 = (bf16[256,1024]{1,0:T(8,128)(2,1)S(1)}, bf16[256,1024]{1,0:T(8,128)(2,1)S(1)}, u32[]{:S(2)}, u32[]{:S(2)}) collective-permute-start(bf16[256,1024]{1,0:T(8,128)(2,1)S(1)} %shard_map.74), channel_id=1, source_target_pairs={{0,2},{1,3},{2,0},{3,1},{4,6},{5,7},{6,4},{7,5},{8,10},{9,11},{10,... | collective-permute-start | bytes 1572872 | tf_op jit(solution)/shard_map/ppermute | solution.py:16
  69.3 9.4 %collective-permute-start.13 = (f32[8,128]{1,0:T(8,128)S(1)}, f32[8,128]{1,0:T(8,128)S(1)}, u32[]{:S(2)}, u32[]{:S(2)}) collective-permute-start(f32[8,128]{1,0:T(8,128)S(1)} %add.43.refs_0_), channel_id=1, source_target_pairs={{0,12},{1,13},{2,14},{3,15},{4,8},{5,9},{6,10},{7,11},{8,4},{9,5},... | collective-permute-start | bytes 12296 | tf_op jit(solution)/shard_map/ppermute | solution.py:16
  74.9 12.7 %collective-permute-start.23 = (bf16[128,1024]{1,0:T(8,128)(2,1)S(1)}, bf16[128,1024]{1,0:T(8,128)(2,1)S(1)}, u32[]{:S(2)}, u32[]{:S(2)}) collective-permute-start(bf16[128,1024]{1,0:T(8,128)(2,1)S(1)} %shard_map.78), channel_id=1, source_target_pairs={{0,4},{1,5},{2,6},{3,7},{4,0},{5,1},{6,2},{7,3},{8,12},{9,13},{10,... | collective-permute-start | bytes 786440 | tf_op jit(solution)/shard_map/ppermute | solution.py:16
  78.7 14.9 %collective-permute-start.21 = (bf16[128,1024]{1,0:T(8,128)(2,1)S(1)}, bf16[128,1024]{1,0:T(8,128)(2,1)S(1)}, u32[]{:S(2)}, u32[]{:S(2)}) collective-permute-start(bf16[128,1024]{1,0:T(8,128)(2,1)S(1)} %shard_map.76), channel_id=1, source_target_pairs={{0,4},{1,5},{2,6},{3,7},{4,0},{5,1},{6,2},{7,3},{8,12},{9,13},{10,... | collective-permute-start | bytes 786440 | tf_op jit(solution)/shard_map/ppermute | solution.py:16

commit v4 on v3

--- a/solution.py
+++ b/solution.py
@@ -58,46 +58,43 @@
         loss = jnp.zeros((8, 128), jnp.float32)
         at, kept = 0, []
         for r0, r1, c0, c1 in plan["new"]:
-            buffer = fresh.at[pl.ds(0, r1 - r0), pl.ds(at, c1 - c0)]
+            buffer = fresh.at[pl.ds(at, c1 - c0), pl.ds(0, r1 - r0)]
             at += c1 - c0
-            kept.append((buffer, coeff.at[pl.ds(r0, r1 - r0), pl.ds(c0, c1 - c0)]))
+            kept.append((buffer, coeff.at[pl.ds(c0, c1 - c0), pl.ds(r0, r1 - r0)]))
+            dots = lax.dot_general(
+                cols[c0:c1, :], rows[r0:r1, :], (((1,), (1,)), ((), ())), preferred_element_type=jnp.float32
+            )
             for cp, cl, j, c_off in plan["col_chunks"]:
                 if cp < c0 or cp >= c1:
                     continue
-                dots = (
-                    lax.dot_general(
-                        rows[r0:r1, :], cols[cp : cp + cl, :], (((1,), (1,)), ((), ())),
-                        preferred_element_type=jnp.float32,
-                    )
-                    * inv_root
-                )
                 target = own ^ plan["col_xors"][j]
                 for rp, rl, i, r_off in plan["row_chunks"]:
                     if rp < r0 or rp >= r1:
                         continue
-                    scores = dots[rp - r0 : rp - r0 + rl]
+                    raw = dots[cp - c0 : cp - c0 + cl, rp - r0 : rp - r0 + rl]
                     pos, neg = tables[i][target], tables[i][size + target]
-                    decay = jnp.exp(-jnp.abs(scores))
+                    decay = jnp.exp2(jnp.abs(raw) * (-inv_root * math.log2(math.e)))
                     whole = 1.0 + decay
-                    large = 1.0 / whole
-                    up = scores >= 0.0
-                    above = jnp.maximum(scores, 0.0)
+                    large = pl.reciprocal(whole)
+                    up = raw >= 0.0
+                    above = jnp.maximum(raw, 0.0)
                     if plan["row_xors"][i] == plan["col_xors"][j]:
-                        later = lax.broadcasted_iota(jnp.int32, scores.shape, 1) + c_off > (
-                            lax.broadcasted_iota(jnp.int32, scores.shape, 0) + r_off
+                        later = lax.broadcasted_iota(jnp.int32, raw.shape, 0) + c_off > (
+                            lax.broadcasted_iota(jnp.int32, raw.shape, 1) + r_off
                         )
                         pos = jnp.where(later, pos, 0.0)
                         soft = jnp.log(whole)
-                        part = fold(pos * (above - scores + soft) + neg * (above + soft), jnp.add)
+                        above, below = above * inv_root, (above - raw) * inv_root
+                        part = fold(pos * (below + soft) + neg * (above + soft), jnp.add)
                     else:
-                        over, total = fold(above, jnp.add), fold(scores, jnp.add)
+                        over, total = fold(above, jnp.add) * inv_root, fold(raw, jnp.add) * inv_root
                         part = neg * over + pos * (over - total)
                         part = part + (pos + neg) * jnp.log(fold(whole, jnp.multiply))
                     gain, drop = neg * inv_root, pos * inv_root
                     values = (jnp.where(up, gain, -drop) + jnp.where(up, -drop, gain) * decay) * large
                     for k in range(0, part.shape[1], 128):
                         loss = loss + part[:, k : k + 128]
-                    buffer[rp - r0 : rp - r0 + rl, cp - c0 : cp - c0 + cl] = values.astype(jnp.bfloat16)
+                    buffer[cp - c0 : cp - c0 + cl, rp - r0 : rp - r0 + rl] = values.astype(jnp.bfloat16)
         loss_ref[...] = loss
         copies = [pltpu.make_async_copy(s, t, sem.at[n_new + k]) for k, (s, t) in enumerate(kept)]
         for copy in copies:
@@ -120,10 +117,10 @@
                         out[at + a - p0 : at + b - p0, :] = value[a - base : b - base].astype(out.dtype)
                     at += p1 - p0
 
-    finish(row_out, plan["row_outs"], lambda a, b: jnp.dot(
-        coeff[a:b, :], cols[...], preferred_element_type=jnp.float32))
-    finish(col_out, plan["col_outs"], lambda a, b: lax.dot_general(
-        coeff[:, a:b], rows[...], (((0,), (0,)), ((), ())), preferred_element_type=jnp.float32))
+    finish(row_out, plan["row_outs"], lambda a, b: lax.dot_general(
+        coeff[:, a:b], cols[...], (((0,), (0,)), ((), ())), preferred_element_type=jnp.float32))
+    finish(col_out, plan["col_outs"], lambda a, b: jnp.dot(
+        coeff[a:b, :], rows[...], preferred_element_type=jnp.float32))
 
 
 def phase(own, tables, rows, cols, held, row_chunks, col_chunks, row_xors, col_xors, new=(), row_outs=(),
@@ -145,7 +142,7 @@
         if held is not None:
             aliases = {len(args) + k: 1 + k for k in range(3)}
         out_shape += [
-            pltpu.VMEM(shape, jnp.bfloat16) for shape in ((n_row, width), (n_col, width), (n_row, n_col))
+            pltpu.VMEM(shape, jnp.bfloat16) for shape in ((n_row, width), (n_col, width), (n_col, n_row))
         ]
     if held is not None:
         args += [pltpu.with_memory_space_constraint(x, pltpu.VMEM) for x in held]
@@ -166,7 +163,7 @@
             input_output_aliases=aliases,
             scratch_shapes=[
                 pltpu.VMEM(
-                    (max([16] + [r1 - r0 for r0, r1, _, _ in new]), max(128, sum(c1 - c0 for _, _, c0, c1 in new))),
+                    (max(16, sum(c1 - c0 for _, _, c0, c1 in new)), max([128] + [r1 - r0 for r0, r1, _, _ in new])),
                     jnp.bfloat16,
                 ),
                 pltpu.SemaphoreType.DMA((max(1, len(rows) + len(cols) + len(new)),)),
@@ -218,7 +215,6 @@
     n, stores = 64, []
     for starts, out, total in zip(groups, outs, totals):
         parts = [(start, ins.pop(0)) for start in starts]
-        lanes = total.shape[2]
         for r in range(0, out.shape[0], n):
             here = pl.ds(r, n)
             value = sum(
@@ -226,9 +222,8 @@
                 for start, part in parts
                 if start <= r < start + part.shape[0]
             )
-            for k in range(total.shape[1]):
-                total[here, k, :] = value[:, k * lanes : (k + 1) * lanes]
-            stores.append(pltpu.make_async_copy(total.at[here], out.at[here], sem.at[len(stores)]))
+            total[here, :] = value
+            stores.append(pltpu.make_async_copy(total.at[here], out.at[here, 0, :], sem.at[len(stores)]))
             stores[-1].start()
     loss_ref[0] = jnp.sum(sum(loss[...] for loss in losses)) * (1.0 / count)
     for copy in stores:
@@ -236,10 +231,10 @@
 
 
 def finish_sums(groups, losses, length, count):
-    width, lanes = groups[0][0][1].shape[1], 128
+    width = groups[0][0][1].shape[1]
     smem, anywhere, vmem = (pl.BlockSpec(memory_space=m) for m in (pltpu.SMEM, pl.ANY, pltpu.VMEM))
     flat = [*losses, *(part for group in groups for _, part in group)]
-    shape = (length, width // lanes, lanes)
+    shape = (length, 1, width)
     loss, *outs = pl.pallas_call(
         functools.partial(
             finish_kernel, [[start for start, _ in group] for group in groups], len(losses), count
@@ -247,12 +242,12 @@
         in_specs=[vmem] * len(flat),
         out_specs=[smem] + [anywhere] * len(groups),
         out_shape=[jax.ShapeDtypeStruct((1,), jnp.float32)] + [jax.ShapeDtypeStruct(shape, jnp.float32)] * len(groups),
-        scratch_shapes=[pltpu.VMEM(shape, jnp.float32)] * len(groups)
+        scratch_shapes=[pltpu.VMEM((length, width), jnp.float32)] * len(groups)
         + [pltpu.SemaphoreType.DMA((len(groups) * (length // 64),))],
         cost_estimate=pl.CostEstimate(flops=6 * length * width, bytes_accessed=20 * length * width, transcendentals=0),
         compiler_params=pltpu.CompilerParams(vmem_limit_bytes=16 << 20),
     )(*[pltpu.with_memory_space_constraint(x, pltpu.VMEM) for x in flat])
-    return [loss, *(out.reshape(length, 1, width) for out in outs)]
+    return [loss, *outs]
 
 
 def step(states, goals, pos_offset, neg_blocks):
@@ -320,7 +315,6 @@
         list(range(n_block - 1, top, -1)), tables, arrived(last, n_col), held, [(0, n_row, last, n_col)]
     )
     loss = loss_a + loss_b + loss_c + loss_d
-    loss = loss + swap(loss, 1, size)
     _, _, (pair_part,), _ = phase(own, [], {}, {}, held, row_outs=[[(length, n_row)]], **fixed)
 
     back_pair = swap(pair_part, across, size)
@@ -329,6 +323,8 @@
     cross = {k: swap(part, 1, size) for k, part in sides.items()}
     for s in reversed(range(len(inner))):
         loss = loss + swap(loss, inner[s], size)
+        if s == len(inner) - 1:
+            loss = loss + swap(loss, 1, size)
     losses = [loss, swap(loss, across, size)]
     addends = {k: [(own_sums[k], 0), (cross[k], 0)] for k in range(n_block)}
     halves = {(k, o): [] for k in range(n_block) for o in (0, half)}
@@ -343,9 +339,8 @@
                 piece = add(half, *[(b, o) for b, _ in addends[k]], *[(b, 0) for b in halves[k, o]])
                 halves[to, o].append(swap(piece, inner[s], size))
     goal_parts = [(0, block) for block, _ in addends[0]] + [(o, b) for o in (0, half) for b in halves[0, o]]
-    loss_mean, grad_states, grad_goals = finish_sums(
-        [[(0, own_part), (0, back_pair)], goal_parts], losses, length, size * length
-    )
+    _, grad_states = finish_sums([[(0, own_part), (0, back_pair)]], losses[:1], length, size * length)
+    loss_mean, grad_goals = finish_sums([goal_parts], losses, length, size * length)
     return (loss_mean, grad_states, grad_goals)
 
 

time: 96.6 us -> 90.2 us (0.934)
  starting transfers between devices: 32.3 us -> 26.6 us
    ppermute x24, starting transfers between devices: 32.3 us -> 26.6 us  [swap(): lax.ppermute(value, AXIS, [(i, i ^ offset) for i in range(size) if only(i)])]
    pallas_call x1 -> x2, Pallas kernels: 2.81 us -> 3.12 us  [finish_sums(): pl.pallas_call(functools.partial(finish_kernel, [[start for start, _ in g...]
  transfers between devices with their start and end apart: 24 -> 24, of which waited for: 10 -> 7; matrix products, arithmetic and copies ran while one was open for 2% -> 2% of each run, Pallas kernels for 11% -> 13%
where the time goes in v4:
time: 90.2 us; the launch traced here: 90 us
  waiting for transfers between devices  42.6 us (47%)
  starting transfers between devices  26.6 us (29%)
  Pallas kernels  16 us (18%)
  local copies, waits for them, and re-layouts  2.08 us (2%)
  other arithmetic  1.77 us (2%)
    ppermute x24, waiting for transfers between devices, swap(): lax.ppermute(value, AXIS, [(i, i ^ offset) for i in range(size) if only(i)])  42.6 us
    ppermute x24, starting transfers between devices, swap(): lax.ppermute(value, AXIS, [(i, i ^ offset) for i in range(size) if only(i)])  26.6 us
    pallas_call x7, Pallas kernels, phase(): pl.pallas_call(functools.partial(tile_kernel, plan), in_specs=in_specs, o...  12.5 us
    pallas_call x2, Pallas kernels, finish_sums(): pl.pallas_call(functools.partial(finish_kernel, [[start for start, _ in g...  3.12 us
    unnamed x4, local copies, waits for them, and re-layouts  2.08 us
  transfers between devices with their start and end apart: 24, of which 7 were waited for; matrix products, arithmetic and copies ran while one was open for 2% of the time, Pallas kernels for 13%

profile of v4, /device:TPU:0, one launch (start us, length us, event | category | flops | bytes accessed | tf_op | source)
XLA Modules:
  0.0 90.0 jit_solution(5741822776993315525)
XLA Ops:
  0.6 3.1 %collective-permute-start.1 = (bf16[256,1024]{1,0:T(8,128)(2,1)}, bf16[256,1024]{1,0:T(8,128)(2,1)S(1)}, u32[]{:S(2)}, u32[]{:S(2)}) collective-permute-start(bf16[256,1024]{1,0:T(8,128)(2,1)} %bitcast.6), channel_id=1, source_target_pairs={{0,4},{1,5},{2,6},{3,7},{4,0},{5,1},{6,2},{7,3},{8,12},{9,13},{10,... | collective-permute-start | bytes 1572872 | tf_op jit(solution)/shard_map/ppermute | solution.py:16
  3.7 1.5 %collective-permute-start.3 = (bf16[256,1024]{1,0:T(8,128)(2,1)}, bf16[256,1024]{1,0:T(8,128)(2,1)S(1)}, u32[]{:S(2)}, u32[]{:S(2)}) collective-permute-start(bf16[256,1024]{1,0:T(8,128)(2,1)} %bitcast.7), channel_id=1, source_target_pairs={{0,2},{1,3},{2,0},{3,1},{4,6},{5,7},{6,4},{7,5},{8,10},{9,11},{10,... | collective-permute-start | bytes 1572872 | tf_op jit(solution)/shard_map/ppermute | solution.py:16
  5.3 0.7 collective-permute-start.6
  6.0 9.9 %collective-permute-done.1.refs_1_ = bf16[256,1024]{1,0:T(8,128)(2,1)S(1)} collective-permute-done((bf16[256,1024]{1,0:T(8,128)(2,1)}, bf16[256,1024]{1,0:T(8,128)(2,1)S(1)}, u32[]{:S(2)}, u32[]{:S(2)}) %collective-permute-start.1) | collective-permute-done | bytes 524320 | tf_op jit(solution)/shard_map/ppermute | solution.py:16
  15.9 1.7 %collective-permute-start.8 = (bf16[256,1024]{1,0:T(8,128)(2,1)S(1)}, bf16[256,1024]{1,0:T(8,128)(2,1)S(1)}, u32[]{:S(2)}, u32[]{:S(2)}) collective-permute-start(bf16[256,1024]{1,0:T(8,128)(2,1)S(1)} %collective-permute-done.1.refs_1_), channel_id=1, source_target_pairs={{0,2},{1,3},{2,0},{3,1},{4,6},{5,7},{6,4},{7,5},{8,10},{9,11},{10,... | collective-permute-start | bytes 1572872 | tf_op jit(solution)/shard_map/ppermute | solution.py:16
  17.6 0.0 collective-permute-start
  17.6 5.5 %collective-permute-start.7 = (bf16[256,1024]{1,0:T(8,128)(2,1)}, bf16[256,1024]{1,0:T(8,128)(2,1)S(1)}, u32[]{:S(2)}, u32[]{:S(2)}) collective-permute-start(bf16[256,1024]{1,0:T(8,128)(2,1)} %bitcast.11), channel_id=1, source_target_pairs={{0,12},{1,13},{2,14},{3,15},{12,0},{13,1},{14,2},{15,3},{16,28},{1... | collective-permute-start | bytes 1572872 | tf_op jit(solution)/shard_map/ppermute | solution.py:16
  23.1 0.3 collective-permute-start.2
  23.4 0.3 collective-permute-start.4
  23.7 5.3 %collective-permute-done.8.refs_2_ = bf16[256,1024]{1,0:T(8,128)(2,1)S(1)} collective-permute-done((bf16[256,1024]{1,0:T(8,128)(2,1)S(1)}, bf16[256,1024]{1,0:T(8,128)(2,1)S(1)}, u32[]{:S(2)}, u32[]{:S(2)}) %collective-permute-start.8) | collective-permute-done | bytes 524320 | tf_op jit(solution)/shard_map/ppermute | solution.py:16
  29.0 0.7 add_bitcast_fusion
  29.6 0.1 convert_reduce_fusion.1
  29.7 0.7 convert_reduce_fusion
  30.5 0.1 pad_maximum_fusion.refs_0_
  30.5 5.3 %collective-permute-done.7 = bf16[256,1024]{1,0:T(8,128)(2,1)S(1)} collective-permute-done((bf16[256,1024]{1,0:T(8,128)(2,1)}, bf16[256,1024]{1,0:T(8,128)(2,1)S(1)}, u32[]{:S(2)}, u32[]{:S(2)}) %collective-permute-start.7) | collective-permute-done | bytes 524320 | tf_op jit(solution)/shard_map/ppermute | solution.py:16
  35.9 3.5 %collective-permute-start.5 = (f32[32]{0:T(128)S(1)}, f32[32]{0:T(128)S(1)}, u32[]{:S(2)}, u32[]{:S(2)}) collective-permute-start(f32[32]{0:T(128)S(1)} %pad_maximum_fusion.refs_0_), channel_id=1, source_target_pairs={{0,12},{1,13},{2,14},{3,15},{4,8},{5,9},{6,10},{7,11},{8,4},{9,5},... | collective-permute-start | bytes 392 | tf_op jit(solution)/shard_map/ppermute | solution.py:16
  39.4 0.2 add.38.refs_2_
  39.6 0.0 collective-permute-done.refs_3_
  39.6 0.0 copy-start
  39.6 1.0 %copy-done = bf16[256,1,1024]{2,0,1:T(8,128)(2,1)S(1)} copy-done((bf16[256,1,1024]{2,0,1:T(8,128)(2,1)S(1)}, bf16[256,1,1024]{2,0,1:T(8,128)(2,1)}, u32[]{:S(2)}) %copy-start) | copy-done | bytes 524312
  40.7 1.0 %copy-done.1 = bf16[256,1,1024]{2,0,1:T(8,128)(2,1)S(1)} copy-done((bf16[256,1,1024]{2,0,1:T(8,128)(2,1)S(1)}, bf16[256,1,1024]{2,0,1:T(8,128)(2,1)}, u32[]{:S(2)}) %copy-start.1) | copy-done | bytes 524312
  41.7 1.4 %shard_map.67 = (f32[8,128]{1,0:T(8,128)S(1)}, bf16[512,1024]{1,0:T(8,128)(2,1)S(1)}, bf16[2048,1024]{1,0:T(8,128)(2,1)S(1)}, bf16[2048,512]{1,0:T(8,128)(2,1)S(1)}) custom-call(s32[1]{0:T(128)} %bitcast.own_ref, f32[32]{0:T(128)S(1)} %pad_maximum_fusion.refs_0_, bf16[256,1024]{1,0:T(8,128)(2,1)S(1)} %bitcast.12, bf16[256,1024]{1,0:T(8,128)(2,1)S(1)} %bitcast.9, ...), custom_call_target="tpu_custom_call" | custom-call | flops 268435456 | bytes 4194304 | tf_op jit(solution)/shard_map/pallas_call | solution.py:158
  43.1 0.0 collective-permute-done.2.refs_2_
  43.2 1.9 %shard_map.68 = (f32[8,128]{1,0:T(8,128)S(1)}, bf16[512,1024]{1,0:T(8,128)(2,1)S(1)}, bf16[2048,1024]{1,0:T(8,128)(2,1)S(1)}, bf16[2048,512]{1,0:T(8,128)(2,1)S(1)}) custom-call(s32[1]{0:T(128)} %bitcast.own_ref, f32[32]{0:T(128)S(1)} %pad_maximum_fusion.refs_0_, ...), custom_call_target="tpu_custom_call", output_to_operand_aliasing={{1}: (6, {}), {2}: (7, {}), {3}: (8, {})} | custom-call | flops 536870912 | bytes 4194304 | tf_op jit(solution)/shard_map/pallas_call | solution.py:158
  45.0 2.2 %shard_map.69 = (f32[8,128]{1,0:T(8,128)S(1)}, bf16[512,1024]{1,0:T(8,128)(2,1)S(1)}, bf16[2048,1024]{1,0:T(8,128)(2,1)S(1)}, bf16[2048,512]{1,0:T(8,128)(2,1)S(1)}) custom-call(s32[1]{0:T(128)} %bitcast.own_ref, f32[32]{0:T(128)S(1)} %pad_maximum_fusion.refs_0_, ...), custom_call_target="tpu_custom_call", output_to_operand_aliasing={{1}: (4, {}), {2}: (5, {}), {3}: (6, {})} | custom-call | flops 805306368 | bytes 4194304 | tf_op jit(solution)/shard_map/pallas_call | solution.py:158
  47.3 2.6 %shard_map.70 = (f32[8,128]{1,0:T(8,128)S(1)}, bf16[512,1024]{1,0:T(8,128)(2,1)S(1)}, bf16[2048,1024]{1,0:T(8,128)(2,1)S(1)}, bf16[2048,512]{1,0:T(8,128)(2,1)S(...) custom-call(s32[1]{0:T(128)} %bitcast.own_ref, ...), custom_call_target="tpu_custom_call", output_to_operand_aliasing={{1}: (5, {}), {2}: (6, {}), {3}: (7, {})} | custom-call | flops 1073741824 | bytes 4194304 | tf_op jit(solution)/shard_map/pallas_call | solution.py:158
  49.9 0.1 collective-permute-start.18
  49.9 0.7 shard_map.72
  50.7 0.6 collective-permute-start.15
  51.2 2.4 %shard_map.71 = (f32[256,1024]{1,0:T(8,128)S(1)}, bf16[256,1024]{1,0:T(8,128)(2,1)S(1)}, f32[256,1024]{1,0:T(8,128)S(1)}, bf16[256,1024]{1,0:T(8,128)(2,1)S(1)}, f32[256,1024]{1,0:T(8,128)S(1)}) custom-call(s32[1]{0:T(128)} %bitcast.own_ref, bf16[512,1024]{1,0:T(8,128)(2,1)S(1)} %get-tuple-element.44.refs_0_, ...), custom_call_target="tpu_custom_call" | custom-call | flops 2147483648 | bytes 4194304 | tf_op jit(solution)/shard_map/pallas_call | solution.py:158
  53.6 0.1 collective-permute-start.17
  53.7 0.6 collective-permute-start.10
  54.3 3.1 %collective-permute-done.10 = f32[8,128]{1,0:T(8,128)S(1)} collective-permute-done((f32[8,128]{1,0:T(8,128)S(1)}, f32[8,128]{1,0:T(8,128)S(1)}, u32[]{:S(2)}, u32[]{:S(2)}) %collective-permute-start.10) | collective-permute-done | bytes 4128 | tf_op jit(solution)/shard_map/ppermute | solution.py:16
  57.4 1.3 %shard_map.79 = bf16[256,1024]{1,0:T(8,128)(2,1)S(1)} custom-call(s32[1]{0:T(128)} %bitcast.own_ref, bf16[512,1024]{1,0:T(8,128)(2,1)S(1)} %get-tuple-element.44.refs_0_, bf16[2048,1024]{1,0:T(8,128)(2,1)S(1)} %get-tuple-element.45.refs_1_, bf16[2048,512]{1,0:T(8,128)(2,1)S(1)} %get-tuple-element.46.refs_2_), custom_call_target="tpu_custom_call" | custom-call | flops 1073741824 | bytes 4194304 | tf_op jit(solution)/shard_map/pallas_call | solution.py:158
  58.7 0.3 collective-permute-start.23
  59.1 0.6 collective-permute-start.21
  59.8 1.6 %collective-permute-start.19 = (bf16[128,1024]{1,0:T(8,128)(2,1)S(1)}, bf16[128,1024]{1,0:T(8,128)(2,1)S(1)}, u32[]{:S(2)}, u32[]{:S(2)}) collective-permute-start(bf16[128,1024]{1,0:T(8,128)(2,1)S(1)} %shard_map.74), channel_id=1, source_target_pairs={{0,2},{1,3},{2,0},{3,1},{4,6},{5,7},{6,4},{7,5},{8,10},{9,11},{10,... | collective-permute-start | bytes 786440 | tf_op jit(solution)/shard_map/ppermute | solution.py:16
  61.3 0.1 shard_map.73
  61.5 0.6 collective-permute-start.16
  62.0 6.3 %collective-permute-done.21.refs_2_ = bf16[128,1024]{1,0:T(8,128)(2,1)S(1)} collective-permute-done((bf16[128,1024]{1,0:T(8,128)(2,1)S(1)}, bf16[128,1024]{1,0:T(8,128)(2,1)S(1)}, u32[]{:S(2)}, u32[]{:S(2)}) %collective-permute-start.21) | collective-permute-done | bytes 262176 | tf_op jit(solution)/shard_map/ppermute | solution.py:16
  68.4 0.1 shard_map.77
  68.5 5.5 %collective-permute-done.19.refs_2_ = bf16[128,1024]{1,0:T(8,128)(2,1)S(1)} collective-permute-done((bf16[128,1024]{1,0:T(8,128)(2,1)S(1)}, bf16[128,1024]{1,0:T(8,128)(2,1)S(1)}, u32[]{:S(2)}, u32[]{:S(2)}) %collective-permute-start.19) | collective-permute-done | bytes 262176 | tf_op jit(solution)/shard_map/ppermute | solution.py:16
  74.0 0.1 shard_map.75
  74.1 2.1 %collective-permute-start.20 = (bf16[128,1024]{1,0:T(8,128)(2,1)S(1)}, bf16[128,1024]{1,0:T(8,128)(2,1)S(1)}, u32[]{:S(2)}, u32[]{:S(2)}) collective-permute-start(bf16[128,1024]{1,0:T(8,128)(2,1)S(1)} %shard_map.75), channel_id=1, source_target_pairs={{0,4},{1,5},{2,6},{3,7},{4,0},{5,1},{6,2},{7,3},{8,12},{9,13},{10,... | collective-permute-start | bytes 786440 | tf_op jit(solution)/shard_map/ppermute | solution.py:16
  76.2 3.5 %collective-permute-start.13 = (f32[8,128]{1,0:T(8,128)S(1)}, f32[8,128]{1,0:T(8,128)S(1)}, u32[]{:S(2)}, u32[]{:S(2)}) collective-permute-start(f32[8,128]{1,0:T(8,128)S(1)} %add.43.refs_0_), channel_id=1, source_target_pairs={{0,12},{1,13},{2,14},{3,15},{4,8},{5,9},{6,10},{7,11},{8,4},{9,5},... | collective-permute-start | bytes 12296 | tf_op jit(solution)/shard_map/ppermute | solution.py:16
  79.7 1.5 %shard_map.80 = (f32[1]{0:T(128)}, f32[256,1,1024]{2,1,0:T(1,128)}) custom-call(f32[8,128]{1,0:T(8,128)S(1)} %add.43.refs_0_, f32[256,1024]{1,0:T(8,128)S(1)} %get-tuple-element.56.refs_1_, bf16[256,1024]{1,0:T(8,128)(2,1)S(1)} %collective-permute-done.23.refs_2_), custom_call_target="tpu_custom_call" | custom-call | flops 1572864 | bytes 5242880 | tf_op jit(solution)/shard_map/pallas_call | solution.py:238
  81.3 7.1 %collective-permute-done.13.refs_1_ = f32[8,128]{1,0:T(8,128)S(1)} collective-permute-done((f32[8,128]{1,0:T(8,128)S(1)}, f32[8,128]{1,0:T(8,128)S(1)}, u32[]{:S(2)}, u32[]{:S(2)}) %collective-permute-start.13) | collective-permute-done | bytes 4128 | tf_op jit(solution)/shard_map/ppermute | solution.py:16
  88.4 1.6 %shard_map.78 = (f32[1]{0:T(128)}, f32[256,1,1024]{2,1,0:T(1,128)}) custom-call(f32[8,128]{1,0:T(8,128)S(1)} %add.43.refs_0_, f32[8,128]{1,0:T(8,128)S(1)} %collective-permute-done.13.refs_1_, f32[256,1024]{1,0:T(8,128)S(1)} %get-tuple-element.47.refs_2_, bf16[256,1024]{1,0:T(8,128)(2,1)S(1)} %collective-permute-done.14.refs_3_, ...), custom_call_target="tpu_custom_call" | custom-call | flops 1572864 | bytes 5242880 | tf_op jit(solution)/shard_map/pallas_call | solution.py:238
  (27 shorter events, 0.2 us)
Async XLA Ops:
  0.6 15.3 %collective-permute-start.1 = (bf16[256,1024]{1,0:T(8,128)(2,1)}, bf16[256,1024]{1,0:T(8,128)(2,1)S(1)}, u32[]{:S(2)}, u32[]{:S(2)}) collective-permute-start(bf16[256,1024]{1,0:T(8,128)(2,1)} %bitcast.6), channel_id=1, source_target_pairs={{0,4},{1,5},{2,6},{3,7},{4,0},{5,1},{6,2},{7,3},{8,12},{9,13},{10,... | collective-permute-start | bytes 1572872 | tf_op jit(solution)/shard_map/ppermute | solution.py:16
  3.7 19.3 %collective-permute-start.3 = (bf16[256,1024]{1,0:T(8,128)(2,1)}, bf16[256,1024]{1,0:T(8,128)(2,1)S(1)}, u32[]{:S(2)}, u32[]{:S(2)}) collective-permute-start(bf16[256,1024]{1,0:T(8,128)(2,1)} %bitcast.7), channel_id=1, source_target_pairs={{0,2},{1,3},{2,0},{3,1},{4,6},{5,7},{6,4},{7,5},{8,10},{9,11},{10,... | collective-permute-start | bytes 1572872 | tf_op jit(solution)/shard_map/ppermute | solution.py:16
  5.3 18.1 %collective-permute-start.6 = (bf16[256,1024]{1,0:T(8,128)(2,1)}, bf16[256,1024]{1,0:T(8,128)(2,1)S(1)}, u32[]{:S(2)}, u32[]{:S(2)}) collective-permute-start(bf16[256,1024]{1,0:T(8,128)(2,1)} %bitcast.10), channel_id=1, source_target_pairs={{4,8},{5,9},{6,10},{7,11},{8,4},{9,5},{10,6},{11,7},{20,24},{21,25... | collective-permute-start | bytes 1572872 | tf_op jit(solution)/shard_map/ppermute | solution.py:16
  15.9 13.1 %collective-permute-start.8 = (bf16[256,1024]{1,0:T(8,128)(2,1)S(1)}, bf16[256,1024]{1,0:T(8,128)(2,1)S(1)}, u32[]{:S(2)}, u32[]{:S(2)}) collective-permute-start(bf16[256,1024]{1,0:T(8,128)(2,1)S(1)} %collective-permute-done.1.refs_1_), channel_id=1, source_target_pairs={{0,2},{1,3},{2,0},{3,1},{4,6},{5,7},{6,4},{7,5},{8,10},{9,11},{10,... | collective-permute-start | bytes 1572872 | tf_op jit(solution)/shard_map/ppermute | solution.py:16
  17.6 22.0 %collective-permute-start = (bf16[256,1024]{1,0:T(8,128)(2,1)}, bf16[256,1024]{1,0:T(8,128)(2,1)S(1)}, u32[]{:S(2)}, u32[]{:S(2)}) collective-permute-start(bf16[256,1024]{1,0:T(8,128)(2,1)} %bitcast.8), channel_id=1, source_target_pairs={{0,1},{1,0},{2,3},{3,2},{4,5},{5,4},{6,7},{7,6},{8,9},{9,8},{10,11... | collective-permute-start | bytes 1572872 | tf_op jit(solution)/shard_map/ppermute | solution.py:16
  17.6 18.3 %collective-permute-start.7 = (bf16[256,1024]{1,0:T(8,128)(2,1)}, bf16[256,1024]{1,0:T(8,128)(2,1)S(1)}, u32[]{:S(2)}, u32[]{:S(2)}) collective-permute-start(bf16[256,1024]{1,0:T(8,128)(2,1)} %bitcast.11), channel_id=1, source_target_pairs={{0,12},{1,13},{2,14},{3,15},{12,0},{13,1},{14,2},{15,3},{16,28},{1... | collective-permute-start | bytes 1572872 | tf_op jit(solution)/shard_map/ppermute | solution.py:16
  23.1 20.0 %collective-permute-start.2 = (bf16[256,1024]{1,0:T(8,128)(2,1)S(1)}, bf16[256,1024]{1,0:T(8,128)(2,1)S(1)}, u32[]{:S(2)}, u32[]{:S(2)}) collective-permute-start(bf16[256,1024]{1,0:T(8,128)(2,1)S(1)} %collective-permute-done.1.refs_1_), channel_id=1, source_target_pairs={{0,1},{1,0},{2,3},{3,2},{4,5},{5,4},{6,7},{7,6},{8,9},{9,8},{10,11... | collective-permute-start | bytes 1572872 | tf_op jit(solution)/shard_map/ppermute | solution.py:16
  23.4 19.8 %collective-permute-start.4 = (bf16[256,1024]{1,0:T(8,128)(2,1)S(1)}, bf16[256,1024]{1,0:T(8,128)(2,1)S(1)}, u32[]{:S(2)}, u32[]{:S(2)}) collective-permute-start(bf16[256,1024]{1,0:T(8,128)(2,1)S(1)} %collective-permute-done.3.refs_3_), channel_id=1, source_target_pairs={{0,1},{1,0},{2,3},{3,2},{4,5},{5,4},{6,7},{7,6},{8,9},{9,8},{10,11... | collective-permute-start | bytes 1572872 | tf_op jit(solution)/shard_map/ppermute | solution.py:16
  29.0 18.3 %collective-permute-start.9 = (bf16[256,1024]{1,0:T(8,128)(2,1)S(1)}, bf16[256,1024]{1,0:T(8,128)(2,1)S(1)}, u32[]{:S(2)}, u32[]{:S(2)}) collective-permute-start(bf16[256,1024]{1,0:T(8,128)(2,1)S(1)} %collective-permute-done.8.refs_2_), channel_id=1, source_target_pairs={{0,1},{1,0},{2,3},{3,2},{4,5},{5,4},{6,7},{7,6},{8,9},{9,8},{10,11... | collective-permute-start | bytes 1572872 | tf_op jit(solution)/shard_map/ppermute | solution.py:16
  35.9 9.2 %collective-permute-start.5 = (f32[32]{0:T(128)S(1)}, f32[32]{0:T(128)S(1)}, u32[]{:S(2)}, u32[]{:S(2)}) collective-permute-start(f32[32]{0:T(128)S(1)} %pad_maximum_fusion.refs_0_), channel_id=1, source_target_pairs={{0,12},{1,13},{2,14},{3,15},{4,8},{5,9},{6,10},{7,11},{8,4},{9,5},... | collective-permute-start | bytes 392 | tf_op jit(solution)/shard_map/ppermute | solution.py:16
  39.6 1.0 %copy-start = (bf16[256,1,1024]{2,0,1:T(8,128)(2,1)S(1)}, bf16[256,1,1024]{2,0,1:T(8,128)(2,1)}, u32[]{:S(2)}) copy-start(bf16[256,1,1024]{2,0,1:T(8,128)(2,1)} %param.5) | copy-start | bytes 1572868
  40.7 1.0 %copy-start.1 = (bf16[256,1,1024]{2,0,1:T(8,128)(2,1)S(1)}, bf16[256,1,1024]{2,0,1:T(8,128)(2,1)}, u32[]{:S(2)}) copy-start(bf16[256,1,1024]{2,0,1:T(8,128)(2,1)} %param.4) | copy-start | bytes 1572868
  49.9 9.2 %collective-permute-start.18 = (bf16[256,1024]{1,0:T(8,128)(2,1)S(1)}, bf16[256,1024]{1,0:T(8,128)(2,1)S(1)}, u32[]{:S(2)}, u32[]{:S(2)}) collective-permute-start(bf16[256,1024]{1,0:T(8,128)(2,1)S(1)} %get-tuple-element.54), channel_id=1, source_target_pairs={{0,1},{1,0},{2,3},{3,2},{4,5},{5,4},{6,7},{7,6},{8,9},{9,8},{10,11... | collective-permute-start | bytes 1572872 | tf_op jit(solution)/shard_map/ppermute | solution.py:16
  50.7 10.7 %collective-permute-start.15 = (bf16[256,1024]{1,0:T(8,128)(2,1)S(1)}, bf16[256,1024]{1,0:T(8,128)(2,1)S(1)}, u32[]{:S(2)}, u32[]{:S(2)}) collective-permute-start(bf16[256,1024]{1,0:T(8,128)(2,1)S(1)} %get-tuple-element.50), channel_id=1, source_target_pairs={{0,1},{1,0},{2,3},{3,2},{4,5},{5,4},{6,7},{7,6},{8,9},{9,8},{10,11... | collective-permute-start | bytes 1572872 | tf_op jit(solution)/shard_map/ppermute | solution.py:16
  53.6 7.8 %collective-permute-start.17 = (bf16[256,1024]{1,0:T(8,128)(2,1)S(1)}, bf16[256,1024]{1,0:T(8,128)(2,1)S(1)}, u32[]{:S(2)}, u32[]{:S(2)}) collective-permute-start(bf16[256,1024]{1,0:T(8,128)(2,1)S(1)} %get-tuple-element.52), channel_id=1, source_target_pairs={{0,1},{1,0},{2,3},{3,2},{4,5},{5,4},{6,7},{7,6},{8,9},{9,8},{10,11... | collective-permute-start | bytes 1572872 | tf_op jit(solution)/shard_map/ppermute | solution.py:16
  53.7 3.7 %collective-permute-start.10 = (f32[8,128]{1,0:T(8,128)S(1)}, f32[8,128]{1,0:T(8,128)S(1)}, u32[]{:S(2)}, u32[]{:S(2)}) collective-permute-start(f32[8,128]{1,0:T(8,128)S(1)} %add_add_fusion), channel_id=1, source_target_pairs={{0,2},{1,3},{2,0},{3,1},{4,6},{5,7},{6,4},{7,5},{8,10},{9,11},{10,... | collective-permute-start | bytes 12296 | tf_op jit(solution)/shard_map/ppermute | solution.py:16
  57.4 2.3 %collective-permute-start.11 = (f32[8,128]{1,0:T(8,128)S(1)}, f32[8,128]{1,0:T(8,128)S(1)}, u32[]{:S(2)}, u32[]{:S(2)}) collective-permute-start(f32[8,128]{1,0:T(8,128)S(1)} %add.41), channel_id=1, source_target_pairs={{0,1},{1,0},{2,3},{3,2},{4,5},{5,4},{6,7},{7,6},{8,9},{9,8},{10,11... | collective-permute-start | bytes 12296 | tf_op jit(solution)/shard_map/ppermute | solution.py:16
  58.7 17.5 %collective-permute-start.23 = (bf16[256,1024]{1,0:T(8,128)(2,1)S(1)}, bf16[256,1024]{1,0:T(8,128)(2,1)S(1)}, u32[]{:S(2)}, u32[]{:S(2)}) collective-permute-start(bf16[256,1024]{1,0:T(8,128)(2,1)S(1)} %shard_map.79), channel_id=1, source_target_pairs={{0,12},{1,13},{2,14},{3,15},{4,8},{5,9},{6,10},{7,11},{8,4},{9,5},... | collective-permute-start | bytes 1572872 | tf_op jit(solution)/shard_map/ppermute | solution.py:16
  59.1 9.2 %collective-permute-start.21 = (bf16[128,1024]{1,0:T(8,128)(2,1)S(1)}, bf16[128,1024]{1,0:T(8,128)(2,1)S(1)}, u32[]{:S(2)}, u32[]{:S(2)}) collective-permute-start(bf16[128,1024]{1,0:T(8,128)(2,1)S(1)} %shard_map.76), channel_id=1, source_target_pairs={{0,2},{1,3},{2,0},{3,1},{4,6},{5,7},{6,4},{7,5},{8,10},{9,11},{10,... | collective-permute-start | bytes 786440 | tf_op jit(solution)/shard_map/ppermute | solution.py:16
  59.8 14.2 %collective-permute-start.19 = (bf16[128,1024]{1,0:T(8,128)(2,1)S(1)}, bf16[128,1024]{1,0:T(8,128)(2,1)S(1)}, u32[]{:S(2)}, u32[]{:S(2)}) collective-permute-start(bf16[128,1024]{1,0:T(8,128)(2,1)S(1)} %shard_map.74), channel_id=1, source_target_pairs={{0,2},{1,3},{2,0},{3,1},{4,6},{5,7},{6,4},{7,5},{8,10},{9,11},{10,... | collective-permute-start | bytes 786440 | tf_op jit(solution)/shard_map/ppermute | solution.py:16
  61.3 27.0 %collective-permute-start.14 = (bf16[256,1024]{1,0:T(8,128)(2,1)S(1)}, bf16[256,1024]{1,0:T(8,128)(2,1)S(1)}, u32[]{:S(2)}, u32[]{:S(2)}) collective-permute-start(bf16[256,1024]{1,0:T(8,128)(2,1)S(1)} %get-tuple-element.48), channel_id=1, source_target_pairs={{0,1},{1,0},{2,3},{3,2},{4,5},{5,4},{6,7},{7,6},{8,9},{9,8},{10,11... | collective-permute-start | bytes 1572872 | tf_op jit(solution)/shard_map/ppermute | solution.py:16
  61.5 26.9 %collective-permute-start.16 = (bf16[256,1024]{1,0:T(8,128)(2,1)S(1)}, bf16[256,1024]{1,0:T(8,128)(2,1)S(1)}, u32[]{:S(2)}, u32[]{:S(2)}) collective-permute-start(bf16[256,1024]{1,0:T(8,128)(2,1)S(1)} %shard_map.73), channel_id=1, source_target_pairs={{0,2},{1,3},{2,0},{3,1},{4,6},{5,7},{6,4},{7,5},{8,10},{9,11},{10,... | collective-permute-start | bytes 1572872 | tf_op jit(solution)/shard_map/ppermute | solution.py:16
  68.4 5.7 %collective-permute-start.12 = (f32[8,128]{1,0:T(8,128)S(1)}, f32[8,128]{1,0:T(8,128)S(1)}, u32[]{:S(2)}, u32[]{:S(2)}) collective-permute-start(f32[8,128]{1,0:T(8,128)S(1)} %add.42), channel_id=1, source_target_pairs={{0,4},{1,5},{2,6},{3,7},{4,0},{5,1},{6,2},{7,3},{8,12},{9,13},{10,... | collective-permute-start | bytes 12296 | tf_op jit(solution)/shard_map/ppermute | solution.py:16
  74.0 14.4 %collective-permute-start.22 = (bf16[128,1024]{1,0:T(8,128)(2,1)S(1)}, bf16[128,1024]{1,0:T(8,128)(2,1)S(1)}, u32[]{:S(2)}, u32[]{:S(2)}) collective-permute-start(bf16[128,1024]{1,0:T(8,128)(2,1)S(1)} %shard_map.77), channel_id=1, source_target_pairs={{0,4},{1,5},{2,6},{3,7},{4,0},{5,1},{6,2},{7,3},{8,12},{9,13},{10,... | collective-permute-start | bytes 786440 | tf_op jit(solution)/shard_map/ppermute | solution.py:16
  74.1 14.3 %collective-permute-start.20 = (bf16[128,1024]{1,0:T(8,128)(2,1)S(1)}, bf16[128,1024]{1,0:T(8,128)(2,1)S(1)}, u32[]{:S(2)}, u32[]{:S(2)}) collective-permute-start(bf16[128,1024]{1,0:T(8,128)(2,1)S(1)} %shard_map.75), channel_id=1, source_target_pairs={{0,4},{1,5},{2,6},{3,7},{4,0},{5,1},{6,2},{7,3},{8,12},{9,13},{10,... | collective-permute-start | bytes 786440 | tf_op jit(solution)/shard_map/ppermute | solution.py:16
  76.2 12.1 %collective-permute-start.13 = (f32[8,128]{1,0:T(8,128)S(1)}, f32[8,128]{1,0:T(8,128)S(1)}, u32[]{:S(2)}, u32[]{:S(2)}) collective-permute-start(f32[8,128]{1,0:T(8,128)S(1)} %add.43.refs_0_), channel_id=1, source_target_pairs={{0,12},{1,13},{2,14},{3,15},{4,8},{5,9},{6,10},{7,11},{8,4},{9,5},... | collective-permute-start | bytes 12296 | tf_op jit(solution)/shard_map/ppermute | solution.py:16
